TPU v7x, 128 devices: a whole 4x4x4 slice. The times are simulated.
128 devices in a mesh: outer: 16 (over x, y), inner: 8 (over z, core).
Axes of the slice: x: 4, y: 4, z: 4, core: 2. Of those that a mesh axis runs over, the one named last changes fastest.
Arguments:
- queries: bfloat16 [24, 131072, 128], P(None, ('outer', 'inner')), may hold values from -6 to 6
- keys: bfloat16 [24, 131072, 128], P(None, ('outer', 'inner')), may hold values from -6 to 6
- values: bfloat16 [24, 131072, 128], P(None, ('outer', 'inner')), may hold values from -6 to 6
- starts: int32 [128], P(('outer', 'inner')), may hold values from 0 to 1024, as said below
- lengths: int32 [128], P(('outer', 'inner')), may hold values from 0 to 65535, as said below
Outputs:
- attended: bfloat16 [24, 131072, 128], P(None, ('outer', 'inner'))
Inputs may be any that keep to these rules, and one draw needn't show every extreme that they name: `starts`: the value 1024 means that no prompt begins in the block; block 0 has a prompt beginning at offset 0; every prompt but the last in the sequence has between 8192 and 65536 positions, so at most one prompt begins in a block. `lengths`: consistent with starts: the number of positions from the beginning of the prompt holding the block's first position up to that position; no prompt has more than 65536 positions.
All inputs are finite; a program needn't handle non-finite values.
Results may differ from a plain program's by a relative error of at most 0.005.
Values sent between devices are 32-bit elements; how exact they have to be, the bound alone decides.
No kernel may reach another device: no remote copies, remote signals or barrier semaphores. Data moves between devices by JAX's collectives and lax.ppermute only.
A program may use at most 128 MiB of HBM per device.

v0:
```python
import math

import jax
import jax.numpy as jnp
from jax import lax
from jax.sharding import PartitionSpec as P


def carried_in(shard, axis, combine, identity):
    length, place = (lax.axis_size(axis), lax.axis_index(axis))
    everything = jax.tree.map(lambda part: lax.all_gather(part, axis), shard)
    start = jax.tree.map(
        lambda part, zero: jnp.broadcast_to(jnp.asarray(zero, part.dtype), part.shape),
        shard,
        identity,
    )

    def turn(k, before):
        reached = k < place
        new = combine(before, jax.tree.map(lambda part: part[k], everything))
        return jax.tree.map(lambda a, b: jnp.where(reached, a, b), new, before)

    return lax.fori_loop(0, length, turn, start)


def broadcast(value, axis, source):
    kept = jnp.where(lax.axis_index(axis) == source, value, 0).astype(value.dtype)
    return lax.psum(kept, axis)


def combine(earlier, later):
    return (
        jnp.where(later[1] > 0.5, later[0], earlier[0] + later[0]),
        jnp.maximum(earlier[1], later[1]),
    )


def shards(queries, keys, values, starts, lengths):
    block_rows = queries.shape[1]
    head_size = queries.shape[2]
    score_scale = 1.0 / math.sqrt(head_size)
    new_start = starts[0]
    length = lengths[0]
    offsets = jnp.arange(block_rows, dtype=jnp.int32)
    begin = jnp.where(new_start < block_rows, new_start, 0)
    kept_rows = (offsets >= begin).astype(jnp.bfloat16)
    states = jnp.einsum(
        "hsd,hse->hde", keys * kept_rows[None, :, None], values, preferred_element_type=jnp.float32
    )
    resets = (new_start < block_rows).astype(jnp.float32).reshape(1)
    own_part = (states, resets)
    identity = (jnp.zeros_like(states), jnp.zeros_like(resets))
    inner_part = carried_in((states, resets), "inner", combine, identity)
    through = combine(inner_part, own_part)
    last_index = lax.axis_size("inner") - 1
    group_sum = (
        broadcast(through[0], "inner", last_index),
        broadcast(through[1], "inner", last_index),
    )
    before = carried_in((group_sum[0], group_sum[1]), "outer", combine, identity)
    carried_sum = combine(before, inner_part)
    carried = carried_sum[0].astype(jnp.bfloat16)
    earlier = offsets < new_start
    counts = jnp.where(earlier, length + offsets + 1, offsets - new_start + 1).astype(jnp.float32)
    allowed = (earlier[:, None] == earlier[None, :]) & (offsets[None, :] <= offsets[:, None])

    def per_head(pieces):
        query_rows, key_rows, value_rows, carried_head = pieces
        scores = jnp.dot(query_rows, key_rows.T, preferred_element_type=jnp.float32) * score_scale
        scores = jnp.where(allowed, scores, 0.0).astype(jnp.bfloat16)
        inside = jnp.dot(scores, value_rows, preferred_element_type=jnp.float32)
        across = jnp.dot(query_rows, carried_head, preferred_element_type=jnp.float32) * score_scale
        across = across * earlier[:, None]
        return ((inside + across) / jnp.sqrt(counts)[:, None]).astype(jnp.bfloat16)

    return lax.map(per_head, (queries, keys, values, carried))


def solution(mesh):
    return jax.shard_map(
        shards,
        mesh=mesh,
        in_specs=(
            P(None, ("outer", "inner"), None),
            P(None, ("outer", "inner"), None),
            P(None, ("outer", "inner"), None),
            P(("outer", "inner")),
            P(("outer", "inner")),
        ),
        out_specs=P(None, ("outer", "inner"), None),
        check_vma=False,
    )
```

profile of v0, /device:TPU:1, one launch (start us, length us, event | category | flops | bytes accessed | tf_op | source)
XLA Modules:
  0.0 559.3 jit_solution(4673013082450696409)
XLA Ops:
  7.2 8.0 %fusion.37 = f32[24,128,128]{2,1,0:T(8,128)} fusion(bf16[24,1024,128]{2,1,0:T(8,128)(2,1)} %param.13, bf16[24,1024,128]{2,1,0:T(8,128)(2,1)} %param.12, bf16[1024]{0:T(1024)(128)(2,1)S(1)} %fusion.43), kind=kOutput, calls=%fused_computation.38 | convolution fusion | flops 808452096 | bytes 14157824 | tf_op jit(solution)/shard_map/hsd,hse->hde/dot_general | solution.py:47
  16.6 14.5 %all-reduce = f32[8]{0:T(128)S(1)} all-reduce(f32[8]{0:T(128)S(1)} %dynamic-update-slice), channel_id=1, replica_groups=mesh['outer'=16,'inner'=8] {'inner'}, use_global_device_ids=true, to_apply=%add | all-reduce | flops 8 | bytes 64
  31.1 55.4 %all-gather.6.cloned.1.call-done = f32[192,128,128]{2,1,0:T(8,128)} async-done(((f32[24,128,128]{2,1,0:T(8,128)}), f32[192,128,128]{2,1,0:T(8,128)}) %all-gather.6.cloned.1.call-update) | async-done | bytes 12582928 | tf_op jit(solution)/shard_map/all_gather | solution.py:11
  86.5 34.2 %while.44 = (s32[]{:T(128)}, f32[24,128,128]{2,1,0:T(8,128)S(1)}, f32[1]{0:T(128)}, s32[]{:T(128)}, f32[8,1]{0,1:T(1,128)S(1)}, /*index=5*/f32[8,24,128,128]{3,2,1,0:T(8,128)}, s32[]{:T(128)}, s32[]{:T(128)}, f32[1]{0:T(128)}) while((s32[]{:T(128)}, f32[24,128,128]{2,1,0:T(8,128)S(1)}, f32[1]{0:T(128)}, s32[]{:T(128)}, ...), condition=%wide.region_1.2_spmd.clone, body=%wide.region_0.1_spmd.clone.sunk | while | flops 1572871 | bytes 4718756 | solution.py:23
  122.1 62.3 %all-reduce.4.cloned.1.call-done = f32[1,24,128,128]{3,2,1,0:T(8,128)} async-done(((f32[1,24,128,128]{3,2,1,0:T(8,128)}), f32[1,24,128,128]{3,2,1,0:T(8,128)}) %all-reduce.4.cloned.1.call-update) | async-done | bytes 1572880 | tf_op jit(solution)/shard_map/psum | solution.py:28
  185.2 15.6 %psum.14 = f32[1,1]{1,0:T(1,128)} all-reduce(f32[1,1]{1,0:T(1,128)} %bitcast.7), channel_id=1, replica_groups=mesh['outer'=16,'inner'=8] {'inner'}, use_global_device_ids=true, to_apply=%region_3.4 | all-reduce | flops 1 | bytes 8 | tf_op jit(solution)/shard_map/psum | solution.py:28
  202.2 34.4 %all-reduce.1 = f32[16]{0:T(128)S(1)} all-reduce(f32[16]{0:T(128)S(1)} %bitcast_dynamic-update-slice_fusion), channel_id=1, replica_groups=mesh['outer'=16,'inner'=8] {'outer'}, use_global_device_ids=true, to_apply=%add.1 | all-reduce | flops 16 | bytes 128
  236.6 105.9 %all-gather.4.cloned.1.call-done = f32[16,24,128,128]{3,2,1,0:T(8,128)} async-done(((f32[1,24,128,128]{3,2,1,0:T(8,128)}), f32[16,24,128,128]{3,2,1,0:T(8,128)}) %all-gather.4.cloned.1.call-update) | async-done | bytes 25165840 | tf_op jit(solution)/shard_map/all_gather | solution.py:11
  342.4 53.6 %while.45 = (s32[]{:T(128)}, f32[24,128,128]{2,1,0:T(8,128)S(1)}, s32[]{:T(128)}, f32[16,1]{0,1:T(1,128)S(1)}, f32[16,24,128,128]{3,2,1,0:T(8,128)}, /*index=5*/s32[]{:T(128)}, s32[]{:T(128)}) while((s32[]{:T(128)}, f32[24,128,128]{2,1,0:T(8,128)S(1)}, s32[]{:T(128)}, f32[16,1]{0,1:T(1,128)S(1)}, f32[16,24,128,128]{3,2,1,0:T(8,128)}, ...), condition=%wide.region_5.6_spmd.clone, body=%wide.region_4.5_spmd.clone.sunk | while | flops 1572869 | bytes 4718703 | solution.py:23
  343.0 2.7 fusion.60
  346.4 2.7 fusion.60
  349.7 2.7 fusion.60
  353.1 2.7 fusion.60
  356.4 2.7 fusion.60
  359.8 2.7 fusion.60
  363.1 2.7 fusion.60
  366.5 2.7 fusion.60
  369.8 2.7 fusion.60
  373.2 2.7 fusion.60
  376.5 2.7 fusion.60
  379.9 2.7 fusion.60
  383.2 2.7 fusion.60
  386.6 2.7 fusion.60
  390.0 2.7 fusion.60
  393.3 2.7 fusion.60
  397.2 155.6 %while.46 = (s32[]{:T(128)}, bf16[24,1024,128]{2,1,0:T(8,128)(2,1)}, bf16[24,1024,128]{2,1,0:T(8,128)(2,1)}, bf16[24,1024,128]{2,1,0:T(8,128)(2,1)}, bf16[24,102...) while((s32[]{:T(128)}, ...), condition=%wide.region_7.8_spmd.clone.clone, body=%wide.region_6.7_spmd.clone.clone.sunk | while | flops 577250304 | bytes 2413681 | solution.py:76
  397.2 2.5 fusion.66
  403.7 2.5 fusion.66
  410.2 2.5 fusion.66
  416.6 2.5 fusion.66
  423.1 2.5 fusion.66
  429.6 2.5 fusion.66
  436.1 2.5 fusion.66
  442.6 2.5 fusion.66
  449.1 2.5 fusion.66
  455.5 2.5 fusion.66
  462.0 2.5 fusion.66
  468.5 2.5 fusion.66
  475.0 2.5 fusion.66
  481.5 2.5 fusion.66
  488.0 2.5 fusion.66
  494.5 2.5 fusion.66
  500.9 2.5 fusion.66
  507.4 2.5 fusion.66
  513.9 2.5 fusion.66
  520.4 2.5 fusion.66
  526.9 2.5 fusion.66
  533.4 2.5 fusion.66
  (131 shorter events, 139.3 us)
Async XLA Ops:
  6.5 79.9 %all-gather.6.cloned.1.call-start = ((), (), s32[]{:S(2)}) async-start(), calls=%async_computation.2 | async-start | bytes 14155776 | tf_op jit(solution)/shard_map/all_gather | solution.py:11
  7.2 8.1 %copy-start.2 = (u32[128]{0:T(128)S(1)}, u32[128]{0:T(128)}, u32[]{:S(2)}) copy-start(u32[128]{0:T(128)} %constant.119) | copy-start | bytes 1540
  15.2 169.3 %all-reduce.4.cloned.1.call-start = ((), (), s32[]{:S(2)}) async-start(), calls=%async_computation | async-start | bytes 3145728 | tf_op jit(solution)/shard_map/psum | solution.py:28
  86.5 34.2 %copy-start = (f32[24,128,128]{2,1,0:T(8,128)S(1)}, f32[24,128,128]{2,1,0:T(8,128)}, u32[]{:S(2)}) copy-start(f32[24,128,128]{2,1,0:T(8,128)} %fusion.37) | copy-start | bytes 4718596
  122.1 62.5 %copy-start.1 = (u32[128]{0:T(128)S(1)}, u32[128]{0:T(128)}, u32[]{:S(2)}) copy-start(u32[128]{0:T(128)} %constant.124) | copy-start | bytes 1540
  122.1 220.3 %all-gather.4.cloned.1.call-start = ((), (), s32[]{:S(2)}) async-start(), calls=%async_computation.1 | async-start | bytes 26738688 | tf_op jit(solution)/shard_map/all_gather | solution.py:11
Sparse Core Ops, SparseCore 0:
  15.3 71.0 all-gather.5
  122.2 62.2 all-reduce.3
  186.7 155.6 all-gather.3
where the time goes:
time: 562 us; the launch traced here: 559 us
  waiting for transfers between devices  224 us (40%)
  other arithmetic  121 us (22%)
  matrix products  116 us (21%)
  blocking collectives  64.4 us (11%)
  between operations  13.9 us (2%)
  loops' own time  12.2 us (2%)
  local copies, waits for them, and re-layouts  8.72 us (2%)
    all_gather x2, waiting for transfers between devices, carried_in(): everything = jax.tree.map(lambda part: lax.all_gather(part, axis), shard)  161 us
    psum x1, waiting for transfers between devices, broadcast(): return lax.psum(kept, axis)  62.3 us
    select_n x24, other arithmetic, turn(): return jax.tree.map(lambda a, b: jnp.where(reached, a, b), new, before)  61.4 us
    dot_general x24, matrix products, per_head(): inside = jnp.dot(scores, value_rows, preferred_element_type=jnp.float32)  59 us
    unnamed x2, blocking collectives  48.8 us
    dot_general x24, matrix products, per_head(): jnp.dot(query_rows, carried_head, preferred_element_type=jnp.float32)  48.8 us
    sqrt x24, other arithmetic, per_head(): return ((inside + across) / jnp.sqrt(counts)[:, None]).astype(jnp.bfloat16)  31.7 us
    psum x1, blocking collectives, broadcast(): return lax.psum(kept, axis)  15.6 us
  transfers between devices with their start and end apart: 3, of which 3 were waited for; matrix products, arithmetic and copies ran while one was open for 1% of the time, Pallas kernels for 0%

commit v1 on v0

v1 whole, which is shorter than its diff:
```python
import functools
import math

import jax
import jax.numpy as jnp
import numpy as np
from jax import lax
from jax.experimental import pallas as pl
from jax.experimental.pallas import tpu as pltpu
from jax.sharding import Mesh
from jax.sharding import PartitionSpec as P

CHUNK = 256
MIB = 1 << 20


def rows_of(first, shape):
    return first + lax.broadcasted_iota(jnp.int32, shape, 0)


def state_kernel(flagged, heads, scalars, k_ref, v_ref, s_ref, mask_ref):
    step = pl.program_id(0)
    length, width = k_ref.shape[1], k_ref.shape[2]
    start = scalars[0]

    @pl.when(step == 0)
    def _():
        begin = jnp.where(start < length, start, 0)
        kept = rows_of(0, (length, width)) >= begin
        mask_ref[...] = jnp.where(kept, 1.0, 0.0).astype(mask_ref.dtype)
        if flagged:
            flag = jnp.where(start < length, 1.0, 0.0)
            s_ref[-8:, :] = jnp.full((8, width), flag, jnp.float32)

    for h in range(heads):
        state = lax.dot_general(
            k_ref[h] * mask_ref[...],
            v_ref[h],
            (((0,), (0,)), ((), ())),
            preferred_element_type=jnp.float32,
        )
        first = pl.multiple_of((step * heads + h) * width, width)
        s_ref[pl.ds(first, width), :] = state


def block_states(scalars, keys, values, slot, flagged, heads=3):
    count, length, width = keys.shape
    steps = count // 2 // heads
    spec = pl.BlockSpec((heads, length, width), lambda i, s: (s[slot] * steps + i, 0, 0))
    rows = count // 2 * width + (8 if flagged else 0)
    return pl.pallas_call(
        functools.partial(state_kernel, flagged, heads),
        out_shape=jax.ShapeDtypeStruct((rows, width), jnp.float32),
        grid_spec=pltpu.PrefetchScalarGridSpec(
            num_scalar_prefetch=1,
            grid=(steps,),
            in_specs=[spec, spec],
            out_specs=pl.BlockSpec((rows, width), lambda i, s: (0, 0)),
            scratch_shapes=[pltpu.VMEM((length, width), jnp.bfloat16)],
        ),
        compiler_params=pltpu.CompilerParams(vmem_limit_bytes=16 * MIB),
        cost_estimate=pl.CostEstimate(
            flops=count * length * width * width,
            bytes_accessed=count * length * width * 2,
            transcendentals=0,
        ),
        name="states",
    )(scalars, keys, values)


def chip_kernel(scalars, own_ref, got_ref, out_ref):
    first = scalars[2] == 0
    own_reset = jnp.where(scalars[0] < scalars[3], 1.0, 0.0)
    got_reset = got_ref[-8:, :]
    own_part = jnp.where(first, 1.0 - got_reset, 1.0)
    got_part = jnp.where(first, 1.0, 1.0 - own_reset)
    slices, rows, width = out_ref.shape
    data = rows - 8
    own = own_ref[...].reshape(slices * data // 8, 8, width)
    got = got_ref[: slices * data, :].reshape(slices * data // 8, 8, width)
    total = own * own_part[None] + got * got_part
    out_ref[:, :data, :] = total.reshape(slices, data, width)
    mark = jnp.maximum(got_reset, own_reset)
    out_ref[:, data:, :] = jnp.broadcast_to(mark[None], (slices, 8, width))


def chip_states(scalars, own, got, slices):
    rows, width = own.shape
    return pl.pallas_call(
        chip_kernel,
        out_shape=jax.ShapeDtypeStruct((slices, rows // slices + 8, width), jnp.float32),
        in_specs=[
            pl.BlockSpec(memory_space=pltpu.SMEM),
            pl.BlockSpec(memory_space=pltpu.VMEM),
            pl.BlockSpec(memory_space=pltpu.VMEM),
        ],
        out_specs=pl.BlockSpec(memory_space=pltpu.VMEM),
        compiler_params=pltpu.CompilerParams(vmem_limit_bytes=16 * MIB),
        name="chip_states",
    )(scalars, own, got)


def scan_kernel(part_ref, out_ref):
    slices, data, width = out_ref.shape

    def turn(c, before):
        out_ref[c] = before
        part = part_ref[c]
        reset = part[data:, :]
        kept = before.reshape(data // 8, 8, width) * (1.0 - reset)[None]
        return kept.reshape(data, width) + part[:data, :]

    lax.fori_loop(0, slices, turn, jnp.zeros((data, width), jnp.float32), unroll=8)


def scan_chips(parts):
    slices, rows, width = parts.shape
    return pl.pallas_call(
        scan_kernel,
        out_shape=jax.ShapeDtypeStruct((slices, rows - 8, width), jnp.float32),
        in_specs=[pl.BlockSpec(memory_space=pltpu.VMEM)],
        out_specs=pl.BlockSpec(memory_space=pltpu.VMEM),
        compiler_params=pltpu.CompilerParams(vmem_limit_bytes=16 * MIB),
        name="scan_chips",
    )(parts)


def core_kernel(scalars, before_ref, own_ref, got_ref, mine_ref, send_ref):
    first = scalars[2] == 0
    rows, width = own_ref.shape
    shape = (rows // 8, 8, width)
    own_reset = jnp.where(scalars[0] < scalars[3], 1.0, 0.0)
    reset = jnp.where(first, own_reset, got_ref[rows:, :])
    before = before_ref[...].reshape(shape)
    state = jnp.where(first, own_ref[...], got_ref[:rows, :]).reshape(shape)
    after = before * (1.0 - reset)[None] + state
    mine_ref[...] = jnp.where(first, before, after).reshape(rows, width)
    send_ref[...] = jnp.where(first, after, before).reshape(rows, width)


def core_carried(scalars, before, own, got):
    rows, width = own.shape
    out = jax.ShapeDtypeStruct((rows, width), jnp.float32)
    vmem = pl.BlockSpec(memory_space=pltpu.VMEM)
    return pl.pallas_call(
        core_kernel,
        out_shape=(out, out),
        in_specs=[pl.BlockSpec(memory_space=pltpu.SMEM), vmem, vmem, vmem],
        out_specs=(vmem, vmem),
        compiler_params=pltpu.CompilerParams(vmem_limit_bytes=16 * MIB),
        name="core_carried",
    )(scalars, before, own, got)


def inverse_roots(start, length, rows, width):
    offsets = rows_of(0, (rows, width))
    counts = jnp.where(offsets < start, length + offsets + 1, offsets - start + 1)
    return 1.0 / jnp.sqrt(counts.astype(jnp.float32))


def inside_kernel(
    heads, scale, scalars, q_ref, k_ref, v_ref, o_ref, pair_ref, query_ref, key_ref, root_ref
):
    start, length = scalars[0], scalars[1]
    rows, width = q_ref.shape[1], q_ref.shape[2]
    chunks = rows // CHUNK

    @pl.when(pl.program_id(0) == 0)
    def _():
        root_ref[...] = inverse_roots(start, length, rows, width)
        for i in range(chunks):
            low = i * CHUNK
            inner = (start >= low) & (start < low + CHUNK)
            t = rows_of(low, (CHUNK, CHUNK))
            s = low + lax.broadcasted_iota(jnp.int32, (CHUNK, CHUNK), 1)
            allowed = (s <= t) & ((t < start) == (s < start))
            pair_ref[i] = jnp.where(allowed, scale, 0.0)
            t = rows_of(low, (CHUNK, width))
            cut = jnp.where(inner, start, low + CHUNK)
            query_ref[i] = jnp.where(t < cut, 1.0, 0.0)
            begin = jnp.where(inner, start, low)
            key_ref[i] = jnp.where(t >= begin, 1.0, 0.0).astype(key_ref.dtype)

    for h in range(heads):
        state = None
        for i in range(chunks):
            low = i * CHUNK
            here = slice(low, low + CHUNK)
            q, k, v = q_ref[h, here, :], k_ref[h, here, :], v_ref[h, here, :]
            scores = lax.dot_general(
                q, k, (((1,), (1,)), ((), ())), preferred_element_type=jnp.float32
            )
            scores = (scores * pair_ref[i]).astype(jnp.bfloat16)
            total = jnp.dot(scores, v, preferred_element_type=jnp.float32)
            if i > 0:
                past = (state * scale).astype(jnp.bfloat16)
                total += jnp.dot(q, past, preferred_element_type=jnp.float32) * query_ref[i]
            o_ref[h, here, :] = (total * root_ref[here, :]).astype(o_ref.dtype)
            if i < chunks - 1:
                new = lax.dot_general(
                    k * key_ref[i],
                    v,
                    (((0,), (0,)), ((), ())),
                    preferred_element_type=jnp.float32,
                )
                inner = (start >= low) & (start < low + CHUNK)
                state = new if i == 0 else new + state * jnp.where(inner, 0.0, 1.0)


def inside(scalars, queries, keys, values, scale, heads=2):
    count, rows, width = queries.shape
    chunks = rows // CHUNK
    spec = pl.BlockSpec((heads, rows, width), lambda i, s: (i, 0, 0))
    return pl.pallas_call(
        functools.partial(inside_kernel, heads, scale),
        out_shape=jax.ShapeDtypeStruct(queries.shape, jnp.float32),
        grid_spec=pltpu.PrefetchScalarGridSpec(
            num_scalar_prefetch=1,
            grid=(count // heads,),
            in_specs=[spec, spec, spec],
            out_specs=spec,
            scratch_shapes=[
                pltpu.VMEM((chunks, CHUNK, CHUNK), jnp.float32),
                pltpu.VMEM((chunks, CHUNK, width), jnp.float32),
                pltpu.VMEM((chunks, CHUNK, width), jnp.bfloat16),
                pltpu.VMEM((rows, width), jnp.float32),
            ],
        ),
        compiler_params=pltpu.CompilerParams(vmem_limit_bytes=24 * MIB),
        cost_estimate=pl.CostEstimate(
            flops=count * rows * width * (4 * CHUNK + 4 * width),
            bytes_accessed=count * rows * width * 10,
            transcendentals=0,
        ),
        name="inside",
    )(scalars, queries, keys, values)


def across_kernel(heads, scale, scalars, q_ref, o_ref, c_ref, *rest):
    out_ref, weight_ref = rest[-2:]
    start, length = scalars[0], scalars[1]
    rows, width = q_ref.shape[1], q_ref.shape[2]

    @pl.when(pl.program_id(0) == 0)
    def _():
        weight = inverse_roots(start, length, rows, width) * scale
        weight_ref[...] = jnp.where(rows_of(0, (rows, width)) < start, weight, 0.0)

    for h in range(heads):
        carried = c_ref[h * width : (h + 1) * width, :].astype(jnp.bfloat16)
        across = jnp.dot(q_ref[h], carried, preferred_element_type=jnp.float32)
        out_ref[h] = (o_ref[h] + across * weight_ref[...]).astype(out_ref.dtype)


def add_across(scalars, queries, partial, carried, slot, scale, before=None, heads=3):
    count, rows, width = queries.shape
    steps = count // 2 // heads
    spec = pl.BlockSpec((heads, rows, width), lambda i, s: (s[slot] * steps + i, 0, 0))
    in_specs = [spec, spec, pl.BlockSpec((heads * width, width), lambda i, s: (i, 0))]
    operands = [scalars, queries, partial, carried]
    aliases = {}
    if before is not None:
        in_specs.append(pl.BlockSpec(memory_space=pl.ANY))
        operands.append(before)
        aliases = {4: 0}
    return pl.pallas_call(
        functools.partial(across_kernel, heads, scale),
        out_shape=jax.ShapeDtypeStruct(queries.shape, jnp.bfloat16),
        grid_spec=pltpu.PrefetchScalarGridSpec(
            num_scalar_prefetch=1,
            grid=(steps,),
            in_specs=in_specs,
            out_specs=spec,
            scratch_shapes=[pltpu.VMEM((rows, width), jnp.float32)],
        ),
        input_output_aliases=aliases,
        compiler_params=pltpu.CompilerParams(vmem_limit_bytes=24 * MIB),
        cost_estimate=pl.CostEstimate(
            flops=count * rows * width * width,
            bytes_accessed=count * rows * width * 4,
            transcendentals=0,
        ),
        name="across",
    )(*operands)


def shards(queries, keys, values, starts, lengths):
    count, rows, width = queries.shape
    scale = 1.0 / math.sqrt(width)
    chips = lax.axis_size("outer") * lax.axis_size("z")
    core = lax.axis_index("core").astype(jnp.int32)
    scalars = jnp.stack([starts[0], lengths[0], core, jnp.int32(rows), 1 - core])
    swap = [(0, 1), (1, 0)]

    theirs = block_states(scalars, keys, values, 4, True)
    got = lax.ppermute(theirs, "core", swap)
    own = block_states(scalars, keys, values, 2, False)
    parts = chip_states(scalars, own, got, chips)
    parts = lax.all_to_all(parts, ("outer", "z"), 0, 0, tiled=True)
    partial = inside(scalars, queries, keys, values, scale)
    befores = scan_chips(parts)
    before = lax.all_to_all(befores, ("outer", "z"), 0, 0, tiled=True)
    before = before.reshape(own.shape)
    mine, send = core_carried(scalars, before, own, got)
    rest = lax.ppermute(send, "core", swap)
    out = add_across(scalars, queries, partial, mine, 2, scale)
    return add_across(scalars, queries, partial, rest, 4, scale, before=out)


def solution(mesh):
    outer, inner = mesh.shape["outer"], mesh.shape["inner"]
    chips = Mesh(np.asarray(mesh.devices).reshape(outer, inner // 2, 2), ("outer", "z", "core"))
    everywhere = ("outer", "z", "core")
    return jax.shard_map(
        shards,
        mesh=chips,
        in_specs=(P(None, everywhere, None),) * 3 + (P(everywhere),) * 2,
        out_specs=P(None, everywhere, None),
        check_vma=False,
    )
```

time: 562 us -> 94.5 us (0.17)
  waiting for transfers between devices: 224 us -> 0.01 us
  other arithmetic: 121 us -> 0.01 us
  matrix products: 116 us -> 0 us
  Pallas kernels: 0 us -> 30.7 us
  blocking collectives: 64.4 us -> 47.2 us
  between operations: 13.9 us -> 1.41 us
  loops' own time: 12.2 us -> 0 us
    all_gather x2 -> x0, waiting for transfers between devices: 161 us -> none  [carried_in(): everything = jax.tree.map(lambda part: lax.all_gather(part, axis), shard)]
    dot_general x49 -> x0, matrix products: 116 us -> none  [the longest x24 59 us: per_head(): inside = jnp.dot(scores, value_rows, preferred_element_type=jnp.float32)]
    psum x1 -> x0, waiting for transfers between devices: 62.3 us -> none  [broadcast(): return lax.psum(kept, axis)]
    select_n x24 -> x0, other arithmetic: 61.4 us -> none  [turn(): return jax.tree.map(lambda a, b: jnp.where(reached, a, b), new, before)]
    unnamed x2 -> x0, blocking collectives: 48.8 us -> none
    all_to_all x0 -> x2, blocking collectives: none -> 47.2 us  [the longest x1 28.4 us: shards(): parts = lax.all_to_all(parts, ('outer', 'z'), 0, 0, tiled=True)]
    sqrt x24 -> x0, other arithmetic: 31.7 us -> none  [per_head(): return ((inside + across) / jnp.sqrt(counts)[:, None]).astype(jnp.bfloat16)]
    pallas_call x0 -> x8, Pallas kernels: none -> 30.7 us  [the longest x1 16.6 us: inside(): pl.pallas_call(functools.partial(inside_kernel, heads, scale), out_shape=...]
  transfers between devices with their start and end apart: 3 -> 2, of which waited for: 3 -> 0; matrix products, arithmetic and copies ran while one was open for 1% -> 0% of each run, Pallas kernels for 0% -> 24%
where the time goes in v1:
time: 94.5 us; the launch traced here: 94.2 us
  blocking collectives  47.2 us (50%)
  Pallas kernels  30.7 us (32%)
  local copies, waits for them, and re-layouts  10.3 us (11%)
  starting transfers between devices  4.57 us (5%)
  between operations  1.41 us (1%)
    all_to_all x1, blocking collectives, shards(): parts = lax.all_to_all(parts, ('outer', 'z'), 0, 0, tiled=True)  28.4 us
    all_to_all x1, blocking collectives, shards(): before = lax.all_to_all(befores, ('outer', 'z'), 0, 0, tiled=True)  18.8 us
    pallas_call x1, Pallas kernels, inside(): pl.pallas_call(functools.partial(inside_kernel, heads, scale), out_shape=...  16.6 us
    unnamed x18, local copies, waits for them, and re-layouts  10.2 us
    pallas_call x2, Pallas kernels, add_across(): pl.pallas_call(functools.partial(across_kernel, heads, scale), out_shape=...  7.67 us
    pallas_call x2, Pallas kernels, block_states(): pl.pallas_call(functools.partial(state_kernel, flagged, heads), out_shape...  4.87 us
    ppermute x1, starting transfers between devices, shards(): rest = lax.ppermute(send, 'core', swap)  3.11 us
  transfers between devices with their start and end apart: 2, of which 0 were waited for; matrix products, arithmetic and copies ran while one was open for 0% of the time, Pallas kernels for 24%

profile of v1, /device:TPU:1, one launch (start us, length us, event | category | flops | bytes accessed | tf_op | source)
XLA Modules:
  0.0 94.2 jit_solution(17179145559222141451)
XLA Ops:
  1.3 0.1 stack.11.scalars
  1.4 0.0 copy-start.1
  1.4 2.8 %copy-done.1 = bf16[24,1024,128]{2,1,0:T(8,128)(2,1)S(1)} copy-done((bf16[24,1024,128]{2,1,0:T(8,128)(2,1)S(1)}, bf16[24,1024,128]{2,1,0:T(8,128)(2,1)}, u32[]{:S(2)}) %copy-start.1) | copy-done | bytes 6291480
  4.2 0.0 copy-start.2
  4.2 2.8 %copy-done.2 = bf16[24,1024,128]{2,1,0:T(8,128)(2,1)S(1)} copy-done((bf16[24,1024,128]{2,1,0:T(8,128)(2,1)S(1)}, bf16[24,1024,128]{2,1,0:T(8,128)(2,1)}, u32[]{:S(2)}) %copy-start.2) | copy-done | bytes 6291480
  7.0 0.0 slice-start
  7.0 0.0 slice-start.2
  7.0 0.0 slice-start.4
  7.0 2.4 %states.3 = f32[1544,128]{1,0:T(8,128)S(1)} custom-call(s32[5]{0:T(128)S(1)} %stack.11.scalars, bf16[24,1024,128]{2,1,0:T(8,128)(2,1)S(1)} %copy-done.1, bf16[24,1024,128]{2,1,0:T(8,128)(2,1)S(1)} %copy-done.2), custom_call_target="tpu_custom_call" | custom-call | flops 402653184 | bytes 6291456 | tf_op jit(solution)/shard_map/states/pallas_call | solution.py:51
  9.4 0.0 slice-start.1
  9.4 0.0 slice-start.3
  9.4 0.0 slice-start.5
  9.4 1.5 %collective-permute-start = (f32[1544,128]{1,0:T(8,128)S(1)}, f32[1544,128]{1,0:T(8,128)S(1)}, u32[]{:S(2)}, u32[]{:S(2)}) collective-permute-start(f32[1544,128]{1,0:T(8,128)S(1)} %states.3), channel_id=1, source_target_pairs={{0,1},{1,0},{2,3},{3,2},{4,5},{5,4},{6,7},{7,6},{8,9},{9,8},{10,11... | collective-permute-start | bytes 2371592 | tf_op jit(solution)/shard_map/ppermute | solution.py:296
  10.9 2.4 %states.2.own_ref = f32[1536,128]{1,0:T(8,128)S(1)} custom-call(s32[5]{0:T(128)S(1)} %stack.11.scalars, bf16[24,1024,128]{2,1,0:T(8,128)(2,1)S(1)} %copy-done.1, bf16[24,1024,128]{2,1,0:T(8,128)(2,1)S(1)} %copy-done.2), custom_call_target="tpu_custom_call" | custom-call | flops 402653184 | bytes 6291456 | tf_op jit(solution)/shard_map/states/pallas_call | solution.py:51
  13.3 0.0 collective-permute-done.got_ref
  13.4 0.7 chip_states.1
  14.0 28.4 %all_to_all.10.part_ref = f32[64,32,128]{2,1,0:T(8,128)S(1)} all-to-all(f32[64,32,128]{2,1,0:T(8,128)S(1)} %chip_states.1), channel_id=1, replica_groups=mesh['outer'=16,'z'=4,'core'=2] {'outer','z'}, dimensions={0} | all-to-all | bytes 2097152 | tf_op jit(solution)/shard_map/all_to_all | solution.py:299
  42.4 0.1 scan_chips.1
  42.5 18.8 %all_to_all.11 = f32[64,24,128]{2,1,0:T(8,128)S(1)} all-to-all(f32[64,24,128]{2,1,0:T(8,128)S(1)} %scan_chips.1), channel_id=1, replica_groups=mesh['outer'=16,'z'=4,'core'=2] {'outer','z'}, dimensions={0} | all-to-all | bytes 1572864 | tf_op jit(solution)/shard_map/all_to_all | solution.py:302
  61.4 0.7 core_carried.1
  62.1 3.1 %collective-permute-start.1 = (f32[1536,128]{1,0:T(8,128)S(1)}, f32[1536,128]{1,0:T(8,128)S(1)}, u32[]{:S(2)}, u32[]{:S(2)}) collective-permute-start(f32[1536,128]{1,0:T(8,128)S(1)} %get-tuple-element.7), channel_id=1, source_target_pairs={{0,1},{1,0},{2,3},{3,2},{4,5},{5,4},{6,7},{7,6},{8,9},{9,8},{10,11... | collective-permute-start | bytes 2359304 | tf_op jit(solution)/shard_map/ppermute | solution.py:305
  65.2 0.0 slice-done
  65.2 0.0 slice-done.2
  65.2 0.0 slice-done.4
  65.2 0.0 slice-done.1
  65.2 0.0 slice-done.3
  65.3 0.0 slice-done.5
  65.3 16.6 %inside.1.o_ref = f32[24,1024,128]{2,1,0:T(8,128)} custom-call(s32[5]{0:T(128)S(1)} %stack.11.scalars, bf16[24,1024,128]{2,1,0:T(8,128)(2,1)S(1)} %bitcast.8, bf16[24,1024,128]{2,1,0:T(8,128)(2,1)S(1)} %bitcast.4, bf16[24,1024,128]{2,1,0:T(8,128)(2,1)S(1)} %bitcast.6), custom_call_target="tpu_custom_call" | custom-call | flops 4831838208 | bytes 31457280 | tf_op jit(solution)/shard_map/inside/pallas_call | solution.py:214
  81.9 0.0 copy-start
  81.9 4.6 %copy-done = f32[24,1024,128]{2,1,0:T(8,128)S(1)} copy-done((f32[24,1024,128]{2,1,0:T(8,128)S(1)}, f32[24,1024,128]{2,1,0:T(8,128)}, u32[]{:S(2)}) %copy-start) | copy-done | bytes 12582936
  86.5 3.8 %across.2.rest_0_ = bf16[24,1024,128]{2,1,0:T(8,128)(2,1)} custom-call(s32[5]{0:T(128)S(1)} %stack.11.scalars, bf16[24,1024,128]{2,1,0:T(8,128)(2,1)S(1)} %bitcast.8, f32[24,1024,128]{2,1,0:T(8,128)S(1)} %copy-done, f32[1536,128]{1,0:T(8,128)S(1)} %get-tuple-element.8.c_ref), custom_call_target="tpu_custom_call" | custom-call | flops 402653184 | bytes 12582912 | tf_op jit(solution)/shard_map/across/pallas_call | solution.py:266
  90.3 0.0 collective-permute-done.1.c_ref
  90.3 3.8 %across.3 = bf16[24,1024,128]{2,1,0:T(8,128)(2,1)} custom-call(s32[5]{0:T(128)S(1)} %stack.11.scalars, bf16[24,1024,128]{2,1,0:T(8,128)(2,1)S(1)} %bitcast.8, f32[24,1024,128]{2,1,0:T(8,128)S(1)} %copy-done, f32[1536,128]{1,0:T(8,128)S(1)} %collective-permute-done.1.c_ref, bf16[24,1024,128]{2,1,0:T(8,128)(2,1)} %across.2.rest_0_), custom_call_target="tpu_custom_call", output_to_operand_aliasing={{}: (4, {})} | custom-call | flops 402653184 | bytes 12582912 | tf_op jit(solution)/shard_map/across/pallas_call | solution.py:266
  (3 shorter events, 0.0 us)
Async XLA Ops:
  1.4 2.8 %copy-start.1 = (bf16[24,1024,128]{2,1,0:T(8,128)(2,1)S(1)}, bf16[24,1024,128]{2,1,0:T(8,128)(2,1)}, u32[]{:S(2)}) copy-start(bf16[24,1024,128]{2,1,0:T(8,128)(2,1)} %k_ref.5) | copy-start | bytes 18874372
  4.2 2.8 %copy-start.2 = (bf16[24,1024,128]{2,1,0:T(8,128)(2,1)S(1)}, bf16[24,1024,128]{2,1,0:T(8,128)(2,1)}, u32[]{:S(2)}) copy-start(bf16[24,1024,128]{2,1,0:T(8,128)(2,1)} %v_ref.5) | copy-start | bytes 18874372
  7.0 58.3 %slice-start = ((s8[6291456]{0:T(1024)(128)(4,1)}), s8[4194304]{0:T(1024)(128)(4,1)S(1)}, s32[]{:S(2)}) async-start(s8[6291456]{0:T(1024)(128)(4,1)} %bitcast.3), calls=%async_computation.2 | async-start | bytes 8388608
  7.0 58.3 %slice-start.2 = ((s8[6291456]{0:T(1024)(128)(4,1)}), s8[4194304]{0:T(1024)(128)(4,1)S(1)}, s32[]{:S(2)}) async-start(s8[6291456]{0:T(1024)(128)(4,1)} %bitcast.5), calls=%async_computation.4 | async-start | bytes 8388608
  7.0 58.3 %slice-start.4 = ((s8[6291456]{0:T(1024)(128)(4,1)}), s8[4194304]{0:T(1024)(128)(4,1)S(1)}, s32[]{:S(2)}) async-start(s8[6291456]{0:T(1024)(128)(4,1)} %bitcast.7), calls=%async_computation.6 | async-start | bytes 8388608
  9.4 55.8 %slice-start.1 = ((s8[6291456]{0:T(1024)(128)(4,1)}), s8[2097152]{0:T(1024)(128)(4,1)S(1)}, s32[]{:S(2)}) async-start(s8[6291456]{0:T(1024)(128)(4,1)} %bitcast.3), calls=%async_computation.3 | async-start | bytes 4194304
  9.4 55.8 %slice-start.3 = ((s8[6291456]{0:T(1024)(128)(4,1)}), s8[2097152]{0:T(1024)(128)(4,1)S(1)}, s32[]{:S(2)}) async-start(s8[6291456]{0:T(1024)(128)(4,1)} %bitcast.5), calls=%async_computation.5 | async-start | bytes 4194304
  9.4 55.8 %slice-start.5 = ((s8[6291456]{0:T(1024)(128)(4,1)}), s8[2097152]{0:T(1024)(128)(4,1)S(1)}, s32[]{:S(2)}) async-start(s8[6291456]{0:T(1024)(128)(4,1)} %bitcast.7), calls=%async_computation.7 | async-start | bytes 4194304
  9.4 3.9 %collective-permute-start = (f32[1544,128]{1,0:T(8,128)S(1)}, f32[1544,128]{1,0:T(8,128)S(1)}, u32[]{:S(2)}, u32[]{:S(2)}) collective-permute-start(f32[1544,128]{1,0:T(8,128)S(1)} %states.3), channel_id=1, source_target_pairs={{0,1},{1,0},{2,3},{3,2},{4,5},{5,4},{6,7},{7,6},{8,9},{9,8},{10,11... | collective-permute-start | bytes 2371592 | tf_op jit(solution)/shard_map/ppermute | solution.py:296
  62.1 28.2 %collective-permute-start.1 = (f32[1536,128]{1,0:T(8,128)S(1)}, f32[1536,128]{1,0:T(8,128)S(1)}, u32[]{:S(2)}, u32[]{:S(2)}) collective-permute-start(f32[1536,128]{1,0:T(8,128)S(1)} %get-tuple-element.7), channel_id=1, source_target_pairs={{0,1},{1,0},{2,3},{3,2},{4,5},{5,4},{6,7},{7,6},{8,9},{9,8},{10,11... | collective-permute-start | bytes 2359304 | tf_op jit(solution)/shard_map/ppermute | solution.py:305
  81.9 4.6 %copy-start = (f32[24,1024,128]{2,1,0:T(8,128)S(1)}, f32[24,1024,128]{2,1,0:T(8,128)}, u32[]{:S(2)}) copy-start(f32[24,1024,128]{2,1,0:T(8,128)} %inside.1.o_ref) | copy-start | bytes 37748740

commit v2 on v1

v2 whole, which is shorter than its diff:
```python
import functools
import math

import jax
import jax.numpy as jnp
import numpy as np
from jax import lax
from jax.experimental import pallas as pl
from jax.experimental.pallas import tpu as pltpu
from jax.sharding import Mesh
from jax.sharding import PartitionSpec as P

CHUNK = 256
MIB = 1 << 20
MARKS = 16


def rows_of(first, shape):
    return first + lax.broadcasted_iota(jnp.int32, shape, 0)


def in_hbm(x):
    return pltpu.with_memory_space_constraint(x, pltpu.HBM)


def in_vmem(x):
    return pltpu.with_memory_space_constraint(x, pltpu.VMEM)


def half_of(other):
    core = lax.axis_index("core")
    return 1 - core if other else core


SCALAR = pl.BlockSpec(memory_space=pltpu.SMEM)
WHOLE = pl.BlockSpec(memory_space=pltpu.VMEM)
ANYWHERE = pl.BlockSpec(memory_space=pl.ANY)


def state_kernel(heads, start_ref, k_ref, v_ref, s_ref, mask_ref):
    step = pl.program_id(0)
    length, width = k_ref.shape[1], k_ref.shape[2]

    @pl.when(step == 0)
    def _():
        start = start_ref[0]
        begin = jnp.where(start < length, start, 0)
        kept = rows_of(0, (length, width)) >= begin
        mask_ref[...] = jnp.where(kept, 1.0, 0.0).astype(mask_ref.dtype)
        reset = jnp.where(start < length, 1.0, 0.0)
        first = jnp.where(lax.axis_index("core") == 0, 1.0, 0.0)
        s_ref[-16:-8, :] = jnp.full((8, width), reset, jnp.float32)
        s_ref[-8:, :] = jnp.full((8, width), first, jnp.float32)

    for h in range(heads):
        state = lax.dot_general(
            k_ref[h] * mask_ref[...],
            v_ref[h],
            (((0,), (0,)), ((), ())),
            preferred_element_type=jnp.float32,
        )
        first = pl.multiple_of((step * heads + h) * width, width)
        s_ref[pl.ds(first, width), :] = state


def block_states(starts, keys, values, other, heads=2):
    count, length, width = keys.shape
    steps = count // 2 // heads
    spec = pl.BlockSpec((heads, length, width), lambda i: (half_of(other) * steps + i, 0, 0))
    rows = count // 2 * width + MARKS
    return pl.pallas_call(
        functools.partial(state_kernel, heads),
        out_shape=pltpu.VMEM((rows, width), jnp.float32),
        grid=(steps,),
        in_specs=[SCALAR, spec, spec],
        out_specs=pl.BlockSpec((rows, width), lambda i: (0, 0)),
        scratch_shapes=[pltpu.VMEM((length, width), jnp.bfloat16)],
        compiler_params=pltpu.CompilerParams(vmem_limit_bytes=12 * MIB),
        cost_estimate=pl.CostEstimate(
            flops=count * length * width * width,
            bytes_accessed=count * length * width * 2,
            transcendentals=0,
        ),
        name="states",
    )(starts, in_hbm(keys), in_hbm(values))


def marks(ref):
    return ref[-16:-8, :], ref[-8:, :]


def tiles(x):
    return x.reshape(x.shape[0] // 8, 8, x.shape[1])


def chip_kernel(own_ref, got_ref, out_ref):
    own_reset, first = marks(own_ref)
    got_reset, _ = marks(got_ref)
    own_part = 1.0 - first * got_reset
    got_part = 1.0 - (1.0 - first) * own_reset
    slices, rows, width = out_ref.shape
    data = slices * (rows - 8)
    total = tiles(own_ref[:data, :]) * own_part[None] + tiles(got_ref[:data, :]) * got_part[None]
    out_ref[:, : rows - 8, :] = total.reshape(slices, rows - 8, width)
    mark = jnp.maximum(got_reset, own_reset)
    out_ref[:, rows - 8 :, :] = jnp.broadcast_to(mark[None], (slices, 8, width))


def chip_states(own, got, slices):
    rows, width = own.shape
    return pl.pallas_call(
        chip_kernel,
        out_shape=pltpu.VMEM((slices, (rows - MARKS) // slices + 8, width), jnp.float32),
        in_specs=[WHOLE, WHOLE],
        out_specs=WHOLE,
        compiler_params=pltpu.CompilerParams(vmem_limit_bytes=8 * MIB),
        name="chip_states",
    )(in_vmem(own), in_vmem(got))


def scan_kernel(part_ref, after_ref, out_ref):
    slices, data, width = out_ref.shape

    def turn(c, before):
        out_ref[c] = before
        part = part_ref[c]
        kept = tiles(before) * (1.0 - part[data:, :])[None]
        return kept.reshape(data, width) + part[:data, :]

    lax.fori_loop(0, slices, turn, jnp.zeros((data, width), jnp.float32), unroll=8)


def scan_chips(parts, after):
    slices, rows, width = parts.shape
    return pl.pallas_call(
        scan_kernel,
        out_shape=pltpu.VMEM((slices, rows - 8, width), jnp.float32),
        in_specs=[WHOLE, ANYWHERE],
        out_specs=WHOLE,
        compiler_params=pltpu.CompilerParams(vmem_limit_bytes=8 * MIB),
        name="scan_chips",
    )(in_vmem(parts), after)


def send_kernel(before_ref, own_ref, out_ref):
    reset, first = marks(own_ref)
    data, width = out_ref.shape
    kept, added = 1.0 - first * reset, first
    total = tiles(before_ref[...]) * kept[None] + tiles(own_ref[:data, :]) * added[None]
    out_ref[...] = total.reshape(data, width)


def carried_to_send(before, own):
    return pl.pallas_call(
        send_kernel,
        out_shape=pltpu.VMEM(before.shape, jnp.float32),
        in_specs=[WHOLE, WHOLE],
        out_specs=WHOLE,
        compiler_params=pltpu.CompilerParams(vmem_limit_bytes=8 * MIB),
        name="carried_to_send",
    )(in_vmem(before), in_vmem(own))


def inside_kernel(
    heads,
    scale,
    start_ref,
    length_ref,
    q_ref,
    k_ref,
    v_ref,
    o_ref,
    weight_ref,
    token_ref,
    pair_ref,
    query_ref,
    key_ref,
    root_ref,
):
    start, length = start_ref[0], length_ref[0]
    rows, width = q_ref.shape[1], q_ref.shape[2]
    chunks = rows // CHUNK

    @pl.when(pl.program_id(0) == 0)
    def _():
        offsets = rows_of(0, (rows, width))
        counts = jnp.where(offsets < start, length + offsets + 1, offsets - start + 1)
        root = 1.0 / jnp.sqrt(counts.astype(jnp.float32))
        root_ref[...] = root
        weight_ref[...] = jnp.where(offsets < start, root * scale, 0.0)
        token_ref[...] = jnp.zeros_like(token_ref)
        for i in range(chunks):
            low = i * CHUNK
            inner = (start >= low) & (start < low + CHUNK)
            t = rows_of(low, (CHUNK, CHUNK))
            s = low + lax.broadcasted_iota(jnp.int32, (CHUNK, CHUNK), 1)
            allowed = (s <= t) & ((t < start) == (s < start))
            pair_ref[i] = jnp.where(allowed, scale, 0.0)
            t = rows_of(low, (CHUNK, width))
            cut = jnp.where(inner, start, low + CHUNK)
            query_ref[i] = jnp.where(t < cut, 1.0, 0.0)
            begin = jnp.where(inner, start, low)
            key_ref[i] = jnp.where(t >= begin, 1.0, 0.0).astype(key_ref.dtype)

    for h in range(heads):
        state = None
        for i in range(chunks):
            low = i * CHUNK
            here = slice(low, low + CHUNK)
            q, k, v = q_ref[h, here, :], k_ref[h, here, :], v_ref[h, here, :]
            scores = lax.dot_general(
                q, k, (((1,), (1,)), ((), ())), preferred_element_type=jnp.float32
            )
            scores = (scores * pair_ref[i]).astype(jnp.bfloat16)
            total = jnp.dot(scores, v, preferred_element_type=jnp.float32)
            if i > 0:
                past = (state * scale).astype(jnp.bfloat16)
                total += jnp.dot(q, past, preferred_element_type=jnp.float32) * query_ref[i]
            o_ref[h, here, :] = (total * root_ref[here, :]).astype(o_ref.dtype)
            if i < chunks - 1:
                new = lax.dot_general(
                    k * key_ref[i],
                    v,
                    (((0,), (0,)), ((), ())),
                    preferred_element_type=jnp.float32,
                )
                inner = (start >= low) & (start < low + CHUNK)
                state = new if i == 0 else new + state * jnp.where(inner, 0.0, 1.0)


def inside(starts, lengths, queries, keys, values, scale, heads=2):
    count, rows, width = queries.shape
    chunks = rows // CHUNK
    steps = count // heads
    spec = pl.BlockSpec((heads, rows, width), lambda i: (i, 0, 0))
    return pl.pallas_call(
        functools.partial(inside_kernel, heads, scale),
        out_shape=(
            jax.ShapeDtypeStruct((count, rows, width), jnp.bfloat16),
            jax.ShapeDtypeStruct((rows, width), jnp.float32),
            jax.ShapeDtypeStruct((8, width), jnp.float32),
        ),
        grid=(steps,),
        in_specs=[SCALAR, SCALAR, spec, spec, spec],
        out_specs=(
            spec,
            pl.BlockSpec((rows, width), lambda i: (0, 0)),
            pl.BlockSpec((8, width), lambda i: (0, 0)),
        ),
        scratch_shapes=[
            pltpu.VMEM((chunks, CHUNK, CHUNK), jnp.float32),
            pltpu.VMEM((chunks, CHUNK, width), jnp.float32),
            pltpu.VMEM((chunks, CHUNK, width), jnp.bfloat16),
            pltpu.VMEM((rows, width), jnp.float32),
        ],
        compiler_params=pltpu.CompilerParams(vmem_limit_bytes=16 * MIB),
        cost_estimate=pl.CostEstimate(
            flops=count * rows * width * (4 * CHUNK + 4 * width),
            bytes_accessed=count * rows * width * 8,
            transcendentals=0,
        ),
        name="inside",
    )(starts, lengths, in_hbm(queries), in_hbm(keys), in_hbm(values))


def final_kernel(other, heads, *refs):
    if other:
        q_ref, o_ref, w_ref, carried_ref, _, out_ref = refs
    else:
        q_ref, o_ref, w_ref, before_ref, got_ref, out_ref = refs
        reset, mate = marks(got_ref)
        kept, added = 1.0 - mate * reset, mate
    width = q_ref.shape[2]
    step = pl.program_id(0)
    nothing = jnp.zeros((width, width), jnp.bfloat16)

    def carried(h):
        first = pl.multiple_of((step * heads + h) * width, width)
        here = pl.ds(first, width)
        if other:
            return carried_ref[here, :].astype(jnp.bfloat16)
        total = tiles(before_ref[here, :]) * kept[None] + tiles(got_ref[here, :]) * added[None]
        return total.reshape(width, width).astype(jnp.bfloat16)

    for h in range(0, heads, 2):
        both = jnp.concatenate(
            [
                jnp.concatenate([carried(h), nothing], axis=1),
                jnp.concatenate([nothing, carried(h + 1)], axis=1),
            ],
            axis=0,
        )
        pair = jnp.concatenate([q_ref[h], q_ref[h + 1]], axis=1)
        across = jnp.dot(pair, both, preferred_element_type=jnp.float32)
        for k in range(2):
            part = across[:, k * width : (k + 1) * width]
            total = o_ref[h + k].astype(jnp.float32) + part * w_ref[...]
            out_ref[h + k] = total.astype(out_ref.dtype)


def finish(queries, partial, weights, carried, other, extra, heads=2):
    count, rows, width = queries.shape
    half = count // 2
    steps = half // heads
    spec = pl.BlockSpec((heads, rows, width), lambda i: (half_of(other) * steps + i, 0, 0))

    def all_of(x):
        return pl.BlockSpec(x.shape, lambda i: (0,) * x.ndim)

    return pl.pallas_call(
        functools.partial(final_kernel, other, heads),
        out_shape=jax.ShapeDtypeStruct(queries.shape, jnp.bfloat16),
        grid=(steps,),
        in_specs=[
            spec,
            spec,
            all_of(weights),
            all_of(carried),
            ANYWHERE if other else all_of(extra),
        ],
        out_specs=spec,
        input_output_aliases={4: 0} if other else {},
        compiler_params=pltpu.CompilerParams(vmem_limit_bytes=16 * MIB),
        cost_estimate=pl.CostEstimate(
            flops=2 * half * rows * width * width,
            bytes_accessed=half * rows * width * 6,
            transcendentals=0,
        ),
        name="finish",
    )(in_hbm(queries), in_hbm(partial), weights, carried, extra)


def shards(queries, keys, values, starts, lengths):
    width = queries.shape[2]
    scale = 1.0 / math.sqrt(width)
    chips = lax.axis_size("outer") * lax.axis_size("z")
    swap = [(0, 1), (1, 0)]

    theirs = block_states(starts, keys, values, True)
    got = lax.ppermute(theirs, "core", swap)
    own = block_states(starts, keys, values, False)
    parts = chip_states(own, got, chips)
    parts = lax.all_to_all(parts, ("outer", "z"), 0, 0, tiled=True)
    partial, weights, done = inside(starts, lengths, queries, keys, values, scale)
    befores = scan_chips(parts, done)
    before = lax.all_to_all(befores, ("outer", "z"), 0, 0, tiled=True)
    before = before.reshape(-1, width)
    send = carried_to_send(before, own)
    carried = lax.ppermute(send, "core", swap)
    out = finish(queries, partial, weights, before, False, got)
    return finish(queries, partial, weights, carried, True, out)


def solution(mesh):
    outer, inner = mesh.shape["outer"], mesh.shape["inner"]
    chips = Mesh(np.asarray(mesh.devices).reshape(outer, inner // 2, 2), ("outer", "z", "core"))
    everywhere = ("outer", "z", "core")
    return jax.shard_map(
        shards,
        mesh=chips,
        in_specs=(P(None, everywhere, None),) * 3 + (P(everywhere),) * 2,
        out_specs=P(None, everywhere, None),
        check_vma=False,
    )
```

time: 94.5 us -> 86.6 us (0.916)
  blocking collectives: 47.2 us -> 24 us
  Pallas kernels: 30.7 us -> 42.5 us
  starting transfers between devices: 4.57 us -> 15.2 us
  local copies, waits for them, and re-layouts: 10.3 us -> 2.64 us
    all_to_all x1 -> x0, blocking collectives: 28.4 us -> none  [shards(): parts = lax.all_to_all(parts, ('outer', 'z'), 0, 0, tiled=True)]
    pallas_call x7, Pallas kernels: 14.1 us -> 25.3 us  [the longest x2 13.2 us: finish(): pl.pallas_call(functools.partial(final_kernel, other, heads), out_shape=j...]
    all_to_all x0 -> x1, starting transfers between devices: none -> 11.2 us  [shards(): parts = lax.all_to_all(parts, ('outer', 'z'), 0, 0, tiled=True)]
    unnamed x18 -> x2, local copies, waits for them, and re-layouts: 10.2 us -> 2.64 us
    all_to_all x1, blocking collectives: 18.8 us -> 24 us  [shards(): before = lax.all_to_all(befores, ('outer', 'z'), 0, 0, tiled=True)]
  transfers between devices with their start and end apart: 2 -> 3, of which waited for: 0 -> 0; matrix products, arithmetic and copies ran while one was open for 0% -> 0% of each run, Pallas kernels for 24% -> 34%
where the time goes in v2:
time: 86.6 us; the launch traced here: 85.7 us
  Pallas kernels  42.5 us (49%)
  blocking collectives  24 us (28%)
  starting transfers between devices  15.2 us (18%)
  local copies, waits for them, and re-layouts  2.64 us (3%)
  between operations  1.36 us (2%)
    all_to_all x1, blocking collectives, shards(): before = lax.all_to_all(befores, ('outer', 'z'), 0, 0, tiled=True)  24 us
    pallas_call x1, Pallas kernels, inside(): pl.pallas_call(functools.partial(inside_kernel, heads, scale), out_shape=...  17.1 us
    pallas_call x2, Pallas kernels, finish(): pl.pallas_call(functools.partial(final_kernel, other, heads), out_shape=j...  13.2 us
    all_to_all x1, starting transfers between devices, shards(): parts = lax.all_to_all(parts, ('outer', 'z'), 0, 0, tiled=True)  11.2 us
    pallas_call x2, Pallas kernels, block_states(): pl.pallas_call(functools.partial(state_kernel, heads), out_shape=pltpu.VM...  10.8 us
    unnamed x2, local copies, waits for them, and re-layouts  2.64 us
    ppermute x1, starting transfers between devices, shards(): carried = lax.ppermute(send, 'core', swap)  2.52 us
  transfers between devices with their start and end apart: 3, of which 0 were waited for; matrix products, arithmetic and copies ran while one was open for 0% of the time, Pallas kernels for 34%

profile of v2, /device:TPU:1, one launch (start us, length us, event | category | flops | bytes accessed | tf_op | source)
XLA Modules:
  0.0 85.7 jit_solution(16544528648370540171)
XLA Ops:
  0.7 5.4 %states.3 = f32[1552,128]{1,0:T(8,128)S(1)} custom-call(s32[1]{0:T(128)S(6)} %copy.8.start_ref, bf16[24,1024,128]{2,1,0:T(8,128)(2,1)} %k_ref.5, bf16[24,1024,128]{2,1,0:T(8,128)(2,1)} %v_ref.5), custom_call_target="tpu_custom_call" | custom-call | flops 402653184 | bytes 6291456 | tf_op jit(solution)/shard_map/states/pallas_call | solution.py:71
  6.1 1.5 %collective-permute-start = (f32[1552,128]{1,0:T(8,128)S(1)}, f32[1552,128]{1,0:T(8,128)S(1)}, u32[]{:S(2)}, u32[]{:S(2)}) collective-permute-start(f32[1552,128]{1,0:T(8,128)S(1)} %states.3), channel_id=1, source_target_pairs={{0,1},{1,0},{2,3},{3,2},{4,5},{5,4},{6,7},{7,6},{8,9},{9,8},{10,11... | collective-permute-start | bytes 2383880 | tf_op jit(solution)/shard_map/ppermute | solution.py:340
  7.5 5.4 %states.2.own_ref = f32[1552,128]{1,0:T(8,128)S(1)} custom-call(s32[1]{0:T(128)S(6)} %copy.8.start_ref, bf16[24,1024,128]{2,1,0:T(8,128)(2,1)} %k_ref.5, bf16[24,1024,128]{2,1,0:T(8,128)(2,1)} %v_ref.5), custom_call_target="tpu_custom_call" | custom-call | flops 402653184 | bytes 6291456 | tf_op jit(solution)/shard_map/states/pallas_call | solution.py:71
  12.9 0.0 collective-permute-done.got_ref.refs_4_
  12.9 1.1 %chip_states.1 = f32[64,32,128]{2,1,0:T(8,128)} custom-call(f32[1552,128]{1,0:T(8,128)S(1)} %states.2.own_ref, f32[1552,128]{1,0:T(8,128)S(1)} %collective-permute-done.got_ref.refs_4_), custom_call_target="tpu_custom_call" | custom-call | tf_op jit(solution)/shard_map/chip_states/pallas_call | solution.py:111
  14.0 11.2 %all-to-all-start = ((f32[64,32,128]{2,1,0:T(8,128)}), f32[64,32,128]{2,1,0:T(8,128)S(1)}, u32[]{:S(2)}, u32[]{:S(2)}) async-start(f32[64,32,128]{2,1,0:T(8,128)} %chip_states.1), calls=%async_computation | async-start | bytes 2097152 | tf_op jit(solution)/shard_map/all_to_all | solution.py:343
  25.9 17.1 %inside.1 = (bf16[24,1024,128]{2,1,0:T(8,128)(2,1)S(1)}, f32[1024,128]{1,0:T(8,128)S(1)}, f32[8,128]{1,0:T(8,128)S(1)}) custom-call(s32[1]{0:T(128)S(6)} %copy.8.start_ref, s32[1]{0:T(128)S(6)} %copy.9.length_ref, bf16[24,1024,128]{2,1,0:T(8,128)(2,1)} %refs_0_.3, bf16[24,1024,128]{2,1,0:T(8,128)(2,1)} %k_ref.5, bf16[24,1024,128]{2,1,0:T(8,128)(2,1)} %v_ref.5), custom_call_target="tpu_custom_call" | custom-call | flops 4831838208 | bytes 25165824 | tf_op jit(solution)/shard_map/inside/pallas_call | solution.py:236
  43.1 0.0 copy-start
  43.1 2.6 %copy-done = bf16[24,1024,128]{2,1,0:T(8,128)(2,1)} copy-done((bf16[24,1024,128]{2,1,0:T(8,128)(2,1)}, bf16[24,1024,128]{2,1,0:T(8,128)(2,1)S(1)}, u32[]{:S(2)}) %copy-start) | copy-done | bytes 6291480
  45.8 0.0 all-to-all-done.part_ref
  45.8 0.1 scan_chips.1
  45.9 24.0 %all_to_all.10 = f32[64,24,128]{2,1,0:T(8,128)S(1)} all-to-all(f32[64,24,128]{2,1,0:T(8,128)S(1)} %scan_chips.1), channel_id=1, replica_groups=mesh['outer'=16,'z'=4,'core'=2] {'outer','z'}, dimensions={0} | all-to-all | bytes 1572864 | tf_op jit(solution)/shard_map/all_to_all | solution.py:346
  69.9 0.1 carried_to_send.1
  70.0 2.5 %collective-permute-start.1 = (f32[1536,128]{1,0:T(8,128)S(1)}, f32[1536,128]{1,0:T(8,128)S(1)}, u32[]{:S(2)}, u32[]{:S(2)}) collective-permute-start(f32[1536,128]{1,0:T(8,128)S(1)} %carried_to_send.1), channel_id=1, source_target_pairs={{0,1},{1,0},{2,3},{3,2},{4,5},{5,4},{6,7},{7,6},{8,9},{9,8},{10,11... | collective-permute-start | bytes 2359304 | tf_op jit(solution)/shard_map/ppermute | solution.py:349
  72.5 6.6 %finish.2.refs_4_ = bf16[24,1024,128]{2,1,0:T(8,128)(2,1)} custom-call(bf16[24,1024,128]{2,1,0:T(8,128)(2,1)} %refs_0_.3, bf16[24,1024,128]{2,1,0:T(8,128)(2,1)} %copy-done, f32[1024,128]{1,0:T(8,128)S(1)} %get-tuple-element.9.refs_2_, f32[1536,128]{1,0:T(8,128)S(1)} %bitcast.2, f32[1552,128]{1,0:T(8,128)S(1)} %collective-permute-done.got_ref.refs_4_), custom_call_target="tpu_custom_call" | custom-call | flops 402653184 | bytes 9437184 | tf_op jit(solution)/shard_map/finish/pallas_call | solution.py:310
  79.1 0.0 collective-permute-done.1.refs_3_
  79.1 6.6 %finish.3 = bf16[24,1024,128]{2,1,0:T(8,128)(2,1)} custom-call(bf16[24,1024,128]{2,1,0:T(8,128)(2,1)} %refs_0_.3, bf16[24,1024,128]{2,1,0:T(8,128)(2,1)} %copy-done, f32[1024,128]{1,0:T(8,128)S(1)} %get-tuple-element.9.refs_2_, f32[1536,128]{1,0:T(8,128)S(1)} %collective-permute-done.1.refs_3_, ...), custom_call_target="tpu_custom_call", output_to_operand_aliasing={{}: (4, {})} | custom-call | flops 402653184 | bytes 9437184 | tf_op jit(solution)/shard_map/finish/pallas_call | solution.py:310
Async XLA Ops:
  6.1 6.8 %collective-permute-start = (f32[1552,128]{1,0:T(8,128)S(1)}, f32[1552,128]{1,0:T(8,128)S(1)}, u32[]{:S(2)}, u32[]{:S(2)}) collective-permute-start(f32[1552,128]{1,0:T(8,128)S(1)} %states.3), channel_id=1, source_target_pairs={{0,1},{1,0},{2,3},{3,2},{4,5},{5,4},{6,7},{7,6},{8,9},{9,8},{10,11... | collective-permute-start | bytes 2383880 | tf_op jit(solution)/shard_map/ppermute | solution.py:340
  14.0 31.7 %all-to-all-start = ((f32[64,32,128]{2,1,0:T(8,128)}), f32[64,32,128]{2,1,0:T(8,128)S(1)}, u32[]{:S(2)}, u32[]{:S(2)}) async-start(f32[64,32,128]{2,1,0:T(8,128)} %chip_states.1), calls=%async_computation | async-start | bytes 2097152 | tf_op jit(solution)/shard_map/all_to_all | solution.py:343
  43.1 2.6 %copy-start = (bf16[24,1024,128]{2,1,0:T(8,128)(2,1)}, bf16[24,1024,128]{2,1,0:T(8,128)(2,1)S(1)}, u32[]{:S(2)}) copy-start(bf16[24,1024,128]{2,1,0:T(8,128)(2,1)S(1)} %get-tuple-element.8.refs_1_) | copy-start | bytes 18874372
  70.0 9.1 %collective-permute-start.1 = (f32[1536,128]{1,0:T(8,128)S(1)}, f32[1536,128]{1,0:T(8,128)S(1)}, u32[]{:S(2)}, u32[]{:S(2)}) collective-permute-start(f32[1536,128]{1,0:T(8,128)S(1)} %carried_to_send.1), channel_id=1, source_target_pairs={{0,1},{1,0},{2,3},{3,2},{4,5},{5,4},{6,7},{7,6},{8,9},{9,8},{10,11... | collective-permute-start | bytes 2359304 | tf_op jit(solution)/shard_map/ppermute | solution.py:349

commit v3 on v2

v3 whole, which is shorter than its diff:
```python
import functools
import math

import jax
import jax.numpy as jnp
import numpy as np
from jax import lax
from jax.experimental import pallas as pl
from jax.experimental.pallas import tpu as pltpu
from jax.sharding import Mesh
from jax.sharding import PartitionSpec as P

CHUNK = 256
MIB = 1 << 20
PIECES = 4
MARKS = 16


def rows_of(first, shape):
    return first + lax.broadcasted_iota(jnp.int32, shape, 0)


def in_hbm(x):
    return pltpu.with_memory_space_constraint(x, pltpu.HBM)


def in_vmem(x):
    return pltpu.with_memory_space_constraint(x, pltpu.VMEM)


def half_of(other):
    core = lax.axis_index("core")
    return 1 - core if other else core


def grouped(count, size):
    return [range(h, min(h + size, count)) for h in range(0, count, size)]


SCALAR = pl.BlockSpec(memory_space=pltpu.SMEM)
WHOLE = pl.BlockSpec(memory_space=pltpu.VMEM)
ANYWHERE = pl.BlockSpec(memory_space=pl.ANY)


def state_kernel(other, start_ref, k_hbm, v_hbm, s_ref, k_ref, v_ref, mask_ref, k_sems, v_sems):
    half, length, width = k_ref.shape
    base = half_of(other) * half
    copies = []
    for h in range(half):
        pair = (
            pltpu.make_async_copy(k_hbm.at[base + h], k_ref.at[h], k_sems.at[h]),
            pltpu.make_async_copy(v_hbm.at[base + h], v_ref.at[h], v_sems.at[h]),
        )
        for copy in pair:
            copy.start()
        copies.append(pair)
    start = start_ref[0]
    begin = jnp.where(start < length, start, 0)
    kept = rows_of(0, (length, width)) >= begin
    mask_ref[...] = jnp.where(kept, 1.0, 0.0).astype(mask_ref.dtype)
    reset = jnp.where(start < length, 1.0, 0.0)
    first = jnp.where(lax.axis_index("core") == 0, 1.0, 0.0)
    s_ref[-16:-8, :] = jnp.full((8, width), reset, jnp.float32)
    s_ref[-8:, :] = jnp.full((8, width), first, jnp.float32)
    for group in grouped(half, 3):
        for h in group:
            for copy in copies[h]:
                copy.wait()
        for h in group:
            s_ref[h * width : (h + 1) * width, :] = jnp.dot(
                k_ref[h].T, v_ref[h] * mask_ref[...], preferred_element_type=jnp.float32
            )


def block_states(starts, keys, values, other):
    count, length, width = keys.shape
    half = count // 2
    rows = half * width + MARKS
    return pl.pallas_call(
        functools.partial(state_kernel, other),
        out_shape=pltpu.VMEM((rows, width), jnp.float32),
        in_specs=[SCALAR, ANYWHERE, ANYWHERE],
        out_specs=WHOLE,
        scratch_shapes=[
            pltpu.VMEM((half, length, width), jnp.bfloat16),
            pltpu.VMEM((half, length, width), jnp.bfloat16),
            pltpu.VMEM((length, width), jnp.bfloat16),
            pltpu.SemaphoreType.DMA((half,)),
            pltpu.SemaphoreType.DMA((half,)),
        ],
        compiler_params=pltpu.CompilerParams(vmem_limit_bytes=16 * MIB),
        cost_estimate=pl.CostEstimate(
            flops=count * length * width * width,
            bytes_accessed=count * length * width * 2,
            transcendentals=0,
        ),
        name="states",
    )(starts, in_hbm(keys), in_hbm(values))


def marks(ref):
    return ref[-16:-8, :], ref[-8:, :]


def tiles(x):
    return x.reshape(x.shape[0] // 8, 8, x.shape[1])


def chip_kernel(own_ref, got_ref, out_hbm, out_ref, sems):
    own_reset, first = marks(own_ref)
    got_reset, _ = marks(got_ref)
    own_part = 1.0 - first * got_reset
    got_part = 1.0 - (1.0 - first) * own_reset
    mark = jnp.maximum(got_reset, own_reset)
    slices, rows, width = out_ref.shape
    data = rows - 8
    group = slices // PIECES
    copies = []
    for n in range(PIECES):
        here = slice(n * group * data, (n + 1) * group * data)
        there = slice(n * group, (n + 1) * group)
        total = tiles(own_ref[here, :]) * own_part[None] + tiles(got_ref[here, :]) * got_part[None]
        out_ref[there, :data, :] = total.reshape(group, data, width)
        out_ref[there, data:, :] = jnp.broadcast_to(mark[None], (group, 8, width))
        copy = pltpu.make_async_copy(out_ref.at[there], out_hbm.at[there], sems.at[n])
        copy.start()
        copies.append(copy)
    for copy in copies:
        copy.wait()


def chip_states(own, got, slices):
    rows, width = own.shape
    shape = (slices, (rows - MARKS) // slices + 8, width)
    return pl.pallas_call(
        chip_kernel,
        out_shape=pltpu.HBM(shape, jnp.float32),
        in_specs=[WHOLE, WHOLE],
        out_specs=ANYWHERE,
        scratch_shapes=[pltpu.VMEM(shape, jnp.float32), pltpu.SemaphoreType.DMA((PIECES,))],
        compiler_params=pltpu.CompilerParams(vmem_limit_bytes=8 * MIB),
        name="chip_states",
    )(in_vmem(own), in_vmem(got))


def scan_kernel(part_ref, after_ref, out_hbm, out_ref, sems):
    slices, data, width = out_ref.shape
    group = slices // PIECES
    before = jnp.zeros((data, width), jnp.float32)
    copies = []
    for n in range(PIECES):

        def turn(c, before, n=n):
            out_ref[n * group + c] = before
            part = part_ref[n * group + c]
            kept = tiles(before) * (1.0 - part[data:, :])[None]
            return kept.reshape(data, width) + part[:data, :]

        before = lax.fori_loop(0, group, turn, before, unroll=8)
        there = slice(n * group, (n + 1) * group)
        copy = pltpu.make_async_copy(out_ref.at[there], out_hbm.at[there], sems.at[n])
        copy.start()
        copies.append(copy)
    for copy in copies:
        copy.wait()


def scan_chips(parts, after):
    slices, rows, width = parts.shape
    shape = (slices, rows - 8, width)
    return pl.pallas_call(
        scan_kernel,
        out_shape=pltpu.HBM(shape, jnp.float32),
        in_specs=[WHOLE, ANYWHERE],
        out_specs=ANYWHERE,
        scratch_shapes=[pltpu.VMEM(shape, jnp.float32), pltpu.SemaphoreType.DMA((PIECES,))],
        compiler_params=pltpu.CompilerParams(vmem_limit_bytes=8 * MIB),
        name="scan_chips",
    )(in_vmem(parts), after)


def send_kernel(before_ref, own_ref, after_ref, out_ref):
    reset, first = marks(own_ref)
    data, width = out_ref.shape
    kept, added = 1.0 - first * reset, first
    total = tiles(before_ref[...]) * kept[None] + tiles(own_ref[:data, :]) * added[None]
    out_ref[...] = total.reshape(data, width)


def carried_to_send(before, own, after):
    return pl.pallas_call(
        send_kernel,
        out_shape=pltpu.VMEM(before.shape, jnp.float32),
        in_specs=[WHOLE, WHOLE, ANYWHERE],
        out_specs=WHOLE,
        compiler_params=pltpu.CompilerParams(vmem_limit_bytes=8 * MIB),
        name="carried_to_send",
    )(in_vmem(before), in_vmem(own), after)


def inside_kernel(
    heads,
    scale,
    start_ref,
    length_ref,
    q_ref,
    k_ref,
    v_ref,
    o_ref,
    weight_ref,
    token_ref,
    pair_ref,
    query_ref,
    key_ref,
    root_ref,
):
    rows, width = q_ref.shape[1], q_ref.shape[2]
    chunks = rows // CHUNK

    @pl.when(pl.program_id(0) == 0)
    def _():
        start, length = start_ref[0], length_ref[0]
        offsets = rows_of(0, (rows, width))
        counts = jnp.where(offsets < start, length + offsets + 1, offsets - start + 1)
        root = 1.0 / jnp.sqrt(counts.astype(jnp.float32))
        root_ref[...] = root
        weight_ref[...] = jnp.where(offsets < start, root * scale, 0.0)
        token_ref[...] = jnp.zeros_like(token_ref)
        for i in range(chunks):
            low = i * CHUNK
            inner = (start >= low) & (start < low + CHUNK)
            t = rows_of(low, (CHUNK, CHUNK))
            s = low + lax.broadcasted_iota(jnp.int32, (CHUNK, CHUNK), 1)
            allowed = (s <= t) & ((t < start) == (s < start))
            pair_ref[i] = jnp.where(allowed, scale, 0.0)
            t = rows_of(low, (CHUNK, width))
            cut = jnp.where(inner, start, low + CHUNK)
            query_ref[i] = jnp.where(t < cut, 1.0, 0.0)
            begin = jnp.where(inner, start, low)
            key_ref[i] = jnp.where(t >= begin, 1.0, 0.0).astype(key_ref.dtype)

    start = start_ref[0]
    for h in range(heads):
        state = None
        for i in range(chunks):
            low = i * CHUNK
            here = slice(low, low + CHUNK)
            q, k, v = q_ref[h, here, :], k_ref[h, here, :], v_ref[h, here, :]
            scores = lax.dot_general(
                q, k, (((1,), (1,)), ((), ())), preferred_element_type=jnp.float32
            )
            scores = (scores * pair_ref[i]).astype(jnp.bfloat16)
            total = jnp.dot(scores, v, preferred_element_type=jnp.float32)
            if i > 0:
                past = (state * scale).astype(jnp.bfloat16)
                total += jnp.dot(q, past, preferred_element_type=jnp.float32) * query_ref[i]
            o_ref[h, here, :] = (total * root_ref[here, :]).astype(o_ref.dtype)
            if i < chunks - 1:
                new = lax.dot_general(
                    k * key_ref[i],
                    v,
                    (((0,), (0,)), ((), ())),
                    preferred_element_type=jnp.float32,
                )
                inner = (start >= low) & (start < low + CHUNK)
                state = new if i == 0 else new + state * jnp.where(inner, 0.0, 1.0)


def inside(starts, lengths, queries, keys, values, scale, other, heads=2):
    count, rows, width = queries.shape
    chunks = rows // CHUNK
    half = count // 2
    steps = half // heads
    given = pl.BlockSpec((heads, rows, width), lambda i: (half_of(other) * steps + i, 0, 0))
    return pl.pallas_call(
        functools.partial(inside_kernel, heads, scale),
        out_shape=(
            pltpu.HBM((half, rows, width), jnp.bfloat16),
            jax.ShapeDtypeStruct((rows, width), jnp.float32),
            jax.ShapeDtypeStruct((8, width), jnp.float32),
        ),
        grid=(steps,),
        in_specs=[SCALAR, SCALAR, given, given, given],
        out_specs=(
            pl.BlockSpec((heads, rows, width), lambda i: (i, 0, 0)),
            pl.BlockSpec((rows, width), lambda i: (0, 0)),
            pl.BlockSpec((8, width), lambda i: (0, 0)),
        ),
        scratch_shapes=[
            pltpu.VMEM((chunks, CHUNK, CHUNK), jnp.float32),
            pltpu.VMEM((chunks, CHUNK, width), jnp.float32),
            pltpu.VMEM((chunks, CHUNK, width), jnp.bfloat16),
            pltpu.VMEM((rows, width), jnp.float32),
        ],
        compiler_params=pltpu.CompilerParams(vmem_limit_bytes=16 * MIB),
        cost_estimate=pl.CostEstimate(
            flops=half * rows * width * (4 * CHUNK + 4 * width),
            bytes_accessed=half * rows * width * 8,
            transcendentals=0,
        ),
        name="inside",
    )(starts, lengths, in_hbm(queries), in_hbm(keys), in_hbm(values))


def final_kernel(other, q_hbm, o_hbm, w_ref, carried_ref, *refs):
    if other:
        _, out_hbm, q_ref, o_ref, made_ref, q_sems, o_sems, out_sems = refs
    else:
        got_ref, out_hbm, q_ref, o_ref, made_ref, q_sems, o_sems, out_sems = refs
        reset, mate = marks(got_ref)
        kept, added = 1.0 - mate * reset, mate
    half, rows, width = q_ref.shape
    base = half_of(other) * half
    loads, stores = [], []
    for h in range(half):
        pair = (
            pltpu.make_async_copy(q_hbm.at[base + h], q_ref.at[h], q_sems.at[h]),
            pltpu.make_async_copy(o_hbm.at[h], o_ref.at[h], o_sems.at[h]),
        )
        for copy in pair:
            copy.start()
        loads.append(pair)
    nothing = jnp.zeros((width, width), jnp.bfloat16)

    def carried(h):
        here = slice(h * width, (h + 1) * width)
        total = carried_ref[here, :]
        if not other:
            total = tiles(total) * kept[None] + tiles(got_ref[here, :]) * added[None]
        return total.reshape(width, width).astype(jnp.bfloat16)

    for group in grouped(half, 4):
        for h in group:
            for copy in loads[h]:
                copy.wait()
        for h in group[::2]:
            both = jnp.concatenate(
                [
                    jnp.concatenate([carried(h), nothing], axis=1),
                    jnp.concatenate([nothing, carried(h + 1)], axis=1),
                ],
                axis=0,
            )
            pair = jnp.concatenate([q_ref[h], q_ref[h + 1]], axis=1)
            across = jnp.dot(pair, both, preferred_element_type=jnp.float32)
            for k in range(2):
                part = across[:, k * width : (k + 1) * width]
                total = o_ref[h + k].astype(jnp.float32) + part * w_ref[...]
                made_ref[h + k] = total.astype(made_ref.dtype)
        for h in group:
            store = pltpu.make_async_copy(made_ref.at[h], out_hbm.at[base + h], out_sems.at[h])
            store.start()
            stores.append(store)
    for store in stores:
        store.wait()


def finish(queries, partial, weights, carried, other, extra):
    count, rows, width = queries.shape
    half = count // 2
    return pl.pallas_call(
        functools.partial(final_kernel, other),
        out_shape=pltpu.HBM(queries.shape, jnp.bfloat16),
        in_specs=[ANYWHERE, ANYWHERE, WHOLE, WHOLE, ANYWHERE if other else WHOLE],
        out_specs=ANYWHERE,
        scratch_shapes=[pltpu.VMEM((half, rows, width), jnp.bfloat16)] * 3
        + [pltpu.SemaphoreType.DMA((half,))] * 3,
        input_output_aliases={4: 0} if other else {},
        compiler_params=pltpu.CompilerParams(vmem_limit_bytes=16 * MIB),
        cost_estimate=pl.CostEstimate(
            flops=2 * half * rows * width * width,
            bytes_accessed=half * rows * width * 6,
            transcendentals=0,
        ),
        name="finish",
    )(
        in_hbm(queries),
        in_hbm(partial),
        in_vmem(weights),
        in_vmem(carried),
        in_hbm(extra) if other else in_vmem(extra),
    )


def shards(queries, keys, values, starts, lengths):
    width = queries.shape[2]
    scale = 1.0 / math.sqrt(width)
    chips = lax.axis_size("outer") * lax.axis_size("z")
    swap = [(0, 1), (1, 0)]

    theirs = block_states(starts, keys, values, True)
    got = lax.ppermute(theirs, "core", swap)
    own = block_states(starts, keys, values, False)
    parts = chip_states(own, got, chips)
    parts = lax.all_to_all(parts, ("outer", "z"), 0, 0, tiled=True)
    mine, weights, done = inside(starts, lengths, queries, keys, values, scale, False)
    befores = scan_chips(parts, done)
    before = lax.all_to_all(befores, ("outer", "z"), 0, 0, tiled=True)
    rest, _, done = inside(starts, lengths, queries, keys, values, scale, True)
    before = before.reshape(-1, width)
    send = carried_to_send(before, own, done)
    carried = lax.ppermute(send, "core", swap)
    out = finish(queries, mine, weights, before, False, got)
    return finish(queries, rest, weights, carried, True, out)


def solution(mesh):
    outer, inner = mesh.shape["outer"], mesh.shape["inner"]
    chips = Mesh(np.asarray(mesh.devices).reshape(outer, inner // 2, 2), ("outer", "z", "core"))
    everywhere = ("outer", "z", "core")
    return jax.shard_map(
        shards,
        mesh=chips,
        in_specs=(P(None, everywhere, None),) * 3 + (P(everywhere),) * 2,
        out_specs=P(None, everywhere, None),
        check_vma=False,
    )
```

time: 86.6 us -> 71.8 us (0.83)
  blocking collectives: 24 us -> 0 us
  waiting for transfers between devices: 0.01 us -> 8.85 us
  starting transfers between devices: 15.2 us -> 21.3 us
  Pallas kernels: 42.5 us -> 39.5 us
  local copies, waits for them, and re-layouts: 2.64 us -> 0 us
    all_to_all x1 -> x0, blocking collectives: 24 us -> none  [shards(): before = lax.all_to_all(befores, ('outer', 'z'), 0, 0, tiled=True)]
    pallas_call x6, Pallas kernels: 25.2 us -> 17.7 us  [the longest x2 8.94 us: finish(): pl.pallas_call(functools.partial(final_kernel, other), out_shape=pltpu.HB...]
    all_to_all x1, waiting for transfers between devices: 0.01 us -> 5.89 us  [shards(): parts = lax.all_to_all(parts, ('outer', 'z'), 0, 0, tiled=True)]
    all_to_all x0 -> x1, starting transfers between devices: none -> 5.28 us  [shards(): before = lax.all_to_all(befores, ('outer', 'z'), 0, 0, tiled=True)]
    pallas_call x1 -> x2, Pallas kernels: 17.1 us -> 21.6 us  [inside(): pl.pallas_call(functools.partial(inside_kernel, heads, scale), out_shape=...]
    all_to_all x0 -> x1, waiting for transfers between devices: none -> 2.96 us  [shards(): before = lax.all_to_all(befores, ('outer', 'z'), 0, 0, tiled=True)]
    unnamed x2 -> x0, local copies, waits for them, and re-layouts: 2.64 us -> none
  transfers between devices with their start and end apart: 3 -> 4, of which waited for: 0 -> 2; matrix products, arithmetic and copies ran while one was open for 0% -> 0% of each run, Pallas kernels for 34% -> 41%
where the time goes in v3:
time: 71.8 us; the launch traced here: 71.2 us
  Pallas kernels  39.5 us (55%)
  starting transfers between devices  21.3 us (30%)
  waiting for transfers between devices  8.85 us (12%)
  between operations  1.54 us (2%)
    pallas_call x2, Pallas kernels, inside(): pl.pallas_call(functools.partial(inside_kernel, heads, scale), out_shape=...  21.6 us
    all_to_all x1, starting transfers between devices, shards(): parts = lax.all_to_all(parts, ('outer', 'z'), 0, 0, tiled=True)  11.3 us
    pallas_call x2, Pallas kernels, finish(): pl.pallas_call(functools.partial(final_kernel, other), out_shape=pltpu.HB...  8.94 us
    pallas_call x2, Pallas kernels, block_states(): pl.pallas_call(functools.partial(state_kernel, other), out_shape=pltpu.VM...  6.79 us
    all_to_all x1, waiting for transfers between devices, shards(): parts = lax.all_to_all(parts, ('outer', 'z'), 0, 0, tiled=True)  5.89 us
    all_to_all x1, starting transfers between devices, shards(): before = lax.all_to_all(befores, ('outer', 'z'), 0, 0, tiled=True)  5.28 us
    ppermute x1, starting transfers between devices, shards(): carried = lax.ppermute(send, 'core', swap)  3.31 us
    all_to_all x1, waiting for transfers between devices, shards(): before = lax.all_to_all(befores, ('outer', 'z'), 0, 0, tiled=True)  2.96 us
  transfers between devices with their start and end apart: 4, of which 2 were waited for; matrix products, arithmetic and copies ran while one was open for 0% of the time, Pallas kernels for 41%

profile of v3, /device:TPU:1, one launch (start us, length us, event | category | flops | bytes accessed | tf_op | source)
XLA Modules:
  0.0 71.2 jit_solution(13133281439531282319)
XLA Ops:
  0.7 3.4 %states.3 = f32[1552,128]{1,0:T(8,128)S(1)} custom-call(s32[1]{0:T(128)S(6)} %copy.8.start_ref, bf16[24,1024,128]{2,1,0:T(8,128)(2,1)} %k_hbm.3, bf16[24,1024,128]{2,1,0:T(8,128)(2,1)} %v_hbm.3), custom_call_target="tpu_custom_call" | custom-call | flops 402653184 | bytes 6291456 | tf_op jit(solution)/shard_map/states/pallas_call | solution.py:79
  4.1 1.5 %collective-permute-start = (f32[1552,128]{1,0:T(8,128)S(1)}, f32[1552,128]{1,0:T(8,128)S(1)}, u32[]{:S(2)}, u32[]{:S(2)}) collective-permute-start(f32[1552,128]{1,0:T(8,128)S(1)} %states.3), channel_id=1, source_target_pairs={{0,1},{1,0},{2,3},{3,2},{4,5},{5,4},{6,7},{7,6},{8,9},{9,8},{10,11... | collective-permute-start | bytes 2383880 | tf_op jit(solution)/shard_map/ppermute | solution.py:392
  5.5 3.4 %states.2.own_ref = f32[1552,128]{1,0:T(8,128)S(1)} custom-call(s32[1]{0:T(128)S(6)} %copy.8.start_ref, bf16[24,1024,128]{2,1,0:T(8,128)(2,1)} %k_hbm.3, bf16[24,1024,128]{2,1,0:T(8,128)(2,1)} %v_hbm.3), custom_call_target="tpu_custom_call" | custom-call | flops 402653184 | bytes 6291456 | tf_op jit(solution)/shard_map/states/pallas_call | solution.py:79
  8.9 0.0 collective-permute-done.got_ref.refs_0_
  8.9 1.0 %chip_states.1 = f32[64,32,128]{2,1,0:T(8,128)} custom-call(f32[1552,128]{1,0:T(8,128)S(1)} %states.2.own_ref, f32[1552,128]{1,0:T(8,128)S(1)} %collective-permute-done.got_ref.refs_0_), custom_call_target="tpu_custom_call" | custom-call | tf_op jit(solution)/shard_map/chip_states/pallas_call | solution.py:135
  10.0 11.3 %all-to-all-start = ((f32[64,32,128]{2,1,0:T(8,128)}), f32[64,32,128]{2,1,0:T(8,128)S(1)}, u32[]{:S(2)}, u32[]{:S(2)}) async-start(f32[64,32,128]{2,1,0:T(8,128)} %chip_states.1), calls=%async_computation | async-start | bytes 2097152 | tf_op jit(solution)/shard_map/all_to_all | solution.py:395
  21.9 10.8 %inside.3 = (bf16[12,1024,128]{2,1,0:T(8,128)(2,1)}, f32[1024,128]{1,0:T(8,128)S(1)}, f32[8,128]{1,0:T(8,128)S(1)}) custom-call(s32[1]{0:T(128)S(6)} %copy.8.start_ref, s32[1]{0:T(128)S(6)} %copy.9.length_ref, bf16[24,1024,128]{2,1,0:T(8,128)(2,1)} %q_hbm.3, bf16[24,1024,128]{2,1,0:T(8,128)(2,1)} %k_hbm.3, bf16[24,1024,128]{2,1,0:T(8,128)(2,1)} %v_hbm.3), custom_call_target="tpu_custom_call" | custom-call | flops 2415919104 | bytes 12582912 | tf_op jit(solution)/shard_map/inside/pallas_call | solution.py:275
  32.7 5.9 %all-to-all-done.part_ref = f32[64,32,128]{2,1,0:T(8,128)S(1)} async-done(((f32[64,32,128]{2,1,0:T(8,128)}), f32[64,32,128]{2,1,0:T(8,128)S(1)}, u32[]{:S(2)}, u32[]{:S(2)}) %all-to-all-start) | async-done | bytes 1048608 | tf_op jit(solution)/shard_map/all_to_all | solution.py:395
  38.6 0.9 %scan_chips.1 = f32[64,24,128]{2,1,0:T(8,128)} custom-call(f32[64,32,128]{2,1,0:T(8,128)S(1)} %all-to-all-done.part_ref, f32[8,128]{1,0:T(8,128)S(1)} %get-tuple-element.12.after_ref), custom_call_target="tpu_custom_call" | custom-call | tf_op jit(solution)/shard_map/scan_chips/pallas_call | solution.py:171
  39.5 5.3 %all-to-all-start.1 = ((f32[64,24,128]{2,1,0:T(8,128)}), f32[64,24,128]{2,1,0:T(8,128)S(1)}, u32[]{:S(2)}, u32[]{:S(2)}) async-start(f32[64,24,128]{2,1,0:T(8,128)} %scan_chips.1), calls=%async_computation.1 | async-start | bytes 1572864 | tf_op jit(solution)/shard_map/all_to_all | solution.py:398
  44.8 10.8 %inside.2 = (bf16[12,1024,128]{2,1,0:T(8,128)(2,1)}, f32[1024,128]{1,0:T(8,128)}, f32[8,128]{1,0:T(8,128)S(1)}) custom-call(s32[1]{0:T(128)S(6)} %copy.8.start_ref, s32[1]{0:T(128)S(6)} %copy.9.length_ref, bf16[24,1024,128]{2,1,0:T(8,128)(2,1)} %q_hbm.3, bf16[24,1024,128]{2,1,0:T(8,128)(2,1)} %k_hbm.3, bf16[24,1024,128]{2,1,0:T(8,128)(2,1)} %v_hbm.3), custom_call_target="tpu_custom_call" | custom-call | flops 2415919104 | bytes 12582912 | tf_op jit(solution)/shard_map/inside/pallas_call | solution.py:275
  55.6 3.0 %all-to-all-done.1 = f32[64,24,128]{2,1,0:T(8,128)S(1)} async-done(((f32[64,24,128]{2,1,0:T(8,128)}), f32[64,24,128]{2,1,0:T(8,128)S(1)}, u32[]{:S(2)}, u32[]{:S(2)}) %all-to-all-start.1) | async-done | bytes 786464 | tf_op jit(solution)/shard_map/all_to_all | solution.py:398
  58.6 0.1 carried_to_send.1
  58.7 3.3 %collective-permute-start.1 = (f32[1536,128]{1,0:T(8,128)S(1)}, f32[1536,128]{1,0:T(8,128)S(1)}, u32[]{:S(2)}, u32[]{:S(2)}) collective-permute-start(f32[1536,128]{1,0:T(8,128)S(1)} %carried_to_send.1), channel_id=1, source_target_pairs={{0,1},{1,0},{2,3},{3,2},{4,5},{5,4},{6,7},{7,6},{8,9},{9,8},{10,11... | collective-permute-start | bytes 2359304 | tf_op jit(solution)/shard_map/ppermute | solution.py:402
  62.0 4.5 %finish.2.refs_0_ = bf16[24,1024,128]{2,1,0:T(8,128)(2,1)} custom-call(bf16[24,1024,128]{2,1,0:T(8,128)(2,1)} %q_hbm.3, bf16[12,1024,128]{2,1,0:T(8,128)(2,1)} %get-tuple-element.14.o_hbm, f32[1024,128]{1,0:T(8,128)S(1)} %get-tuple-element.11.w_ref, f32[1536,128]{1,0:T(8,128)S(1)} %bitcast.2, f32[1552,128]{1,0:T(8,128)S(1)} %collective-permute-done.got_ref.refs_0_), custom_call_target="tpu_custom_call" | custom-call | flops 402653184 | bytes 9437184 | tf_op jit(solution)/shard_map/finish/pallas_call | solution.py:361
  66.5 0.0 collective-permute-done.1.carried_ref
  66.5 4.5 %finish.3 = bf16[24,1024,128]{2,1,0:T(8,128)(2,1)} custom-call(bf16[24,1024,128]{2,1,0:T(8,128)(2,1)} %q_hbm.3, bf16[12,1024,128]{2,1,0:T(8,128)(2,1)} %get-tuple-element.10.o_hbm, f32[1024,128]{1,0:T(8,128)S(1)} %get-tuple-element.11.w_ref, f32[1536,128]{1,0:T(8,128)S(1)} %collective-permute-done.1.carried_ref, ...), custom_call_target="tpu_custom_call", output_to_operand_aliasing={{}: (4, {})} | custom-call | flops 402653184 | bytes 9437184 | tf_op jit(solution)/shard_map/finish/pallas_call | solution.py:361
Async XLA Ops:
  4.1 4.9 %collective-permute-start = (f32[1552,128]{1,0:T(8,128)S(1)}, f32[1552,128]{1,0:T(8,128)S(1)}, u32[]{:S(2)}, u32[]{:S(2)}) collective-permute-start(f32[1552,128]{1,0:T(8,128)S(1)} %states.3), channel_id=1, source_target_pairs={{0,1},{1,0},{2,3},{3,2},{4,5},{5,4},{6,7},{7,6},{8,9},{9,8},{10,11... | collective-permute-start | bytes 2383880 | tf_op jit(solution)/shard_map/ppermute | solution.py:392
  10.0 28.6 %all-to-all-start = ((f32[64,32,128]{2,1,0:T(8,128)}), f32[64,32,128]{2,1,0:T(8,128)S(1)}, u32[]{:S(2)}, u32[]{:S(2)}) async-start(f32[64,32,128]{2,1,0:T(8,128)} %chip_states.1), calls=%async_computation | async-start | bytes 2097152 | tf_op jit(solution)/shard_map/all_to_all | solution.py:395
  39.5 19.1 %all-to-all-start.1 = ((f32[64,24,128]{2,1,0:T(8,128)}), f32[64,24,128]{2,1,0:T(8,128)S(1)}, u32[]{:S(2)}, u32[]{:S(2)}) async-start(f32[64,24,128]{2,1,0:T(8,128)} %scan_chips.1), calls=%async_computation.1 | async-start | bytes 1572864 | tf_op jit(solution)/shard_map/all_to_all | solution.py:398
  58.7 7.8 %collective-permute-start.1 = (f32[1536,128]{1,0:T(8,128)S(1)}, f32[1536,128]{1,0:T(8,128)S(1)}, u32[]{:S(2)}, u32[]{:S(2)}) collective-permute-start(f32[1536,128]{1,0:T(8,128)S(1)} %carried_to_send.1), channel_id=1, source_target_pairs={{0,1},{1,0},{2,3},{3,2},{4,5},{5,4},{6,7},{7,6},{8,9},{9,8},{10,11... | collective-permute-start | bytes 2359304 | tf_op jit(solution)/shard_map/ppermute | solution.py:402

commit v4 on v3

--- a/solution.py
+++ b/solution.py
@@ -106,22 +106,25 @@
     return x.reshape(x.shape[0] // 8, 8, x.shape[1])
 
 
-def chip_kernel(own_ref, got_ref, out_hbm, out_ref, sems):
+def chip_kernel(slices, own_ref, got_ref, out_hbm, out_ref, sems):
     own_reset, first = marks(own_ref)
     got_reset, _ = marks(got_ref)
     own_part = 1.0 - first * got_reset
     got_part = 1.0 - (1.0 - first) * own_reset
     mark = jnp.maximum(got_reset, own_reset)
-    slices, rows, width = out_ref.shape
-    data = rows - 8
+    data = (own_ref.shape[0] - MARKS) // slices
+    rows = data + 1
     group = slices // PIECES
     copies = []
     for n in range(PIECES):
         here = slice(n * group * data, (n + 1) * group * data)
-        there = slice(n * group, (n + 1) * group)
         total = tiles(own_ref[here, :]) * own_part[None] + tiles(got_ref[here, :]) * got_part[None]
-        out_ref[there, :data, :] = total.reshape(group, data, width)
-        out_ref[there, data:, :] = jnp.broadcast_to(mark[None], (group, 8, width))
+        total = total.reshape(group * data, -1)
+        for p in range(group):
+            first_row = (n * group + p) * rows
+            out_ref[first_row : first_row + data, :] = total[p * data : (p + 1) * data, :]
+            out_ref[first_row + data : first_row + rows, :] = mark[:1, :]
+        there = slice(n * group * rows, (n + 1) * group * rows)
         copy = pltpu.make_async_copy(out_ref.at[there], out_hbm.at[there], sems.at[n])
         copy.start()
         copies.append(copy)
@@ -131,9 +134,9 @@
 
 def chip_states(own, got, slices):
     rows, width = own.shape
-    shape = (slices, (rows - MARKS) // slices + 8, width)
-    return pl.pallas_call(
-        chip_kernel,
+    shape = (rows - MARKS + slices, width)
+    return pl.pallas_call(
+        functools.partial(chip_kernel, slices),
         out_shape=pltpu.HBM(shape, jnp.float32),
         in_specs=[WHOLE, WHOLE],
         out_specs=ANYWHERE,
@@ -149,15 +152,12 @@
     before = jnp.zeros((data, width), jnp.float32)
     copies = []
     for n in range(PIECES):
-
-        def turn(c, before, n=n):
-            out_ref[n * group + c] = before
-            part = part_ref[n * group + c]
-            kept = tiles(before) * (1.0 - part[data:, :])[None]
-            return kept.reshape(data, width) + part[:data, :]
-
-        before = lax.fori_loop(0, group, turn, before, unroll=8)
         there = slice(n * group, (n + 1) * group)
+        for c in range(slices)[there]:
+            out_ref[c] = before
+            first = c * (data + 1)
+            reset = part_ref[first + data : first + data + 1, :]
+            before = before * (1.0 - reset) + part_ref[first : first + data, :]
         copy = pltpu.make_async_copy(out_ref.at[there], out_hbm.at[there], sems.at[n])
         copy.start()
         copies.append(copy)
@@ -165,9 +165,9 @@
         copy.wait()
 
 
-def scan_chips(parts, after):
-    slices, rows, width = parts.shape
-    shape = (slices, rows - 8, width)
+def scan_chips(parts, after, slices):
+    rows, width = parts.shape
+    shape = (slices, rows // slices - 1, width)
     return pl.pallas_call(
         scan_kernel,
         out_shape=pltpu.HBM(shape, jnp.float32),
@@ -329,7 +329,7 @@
             total = tiles(total) * kept[None] + tiles(got_ref[here, :]) * added[None]
         return total.reshape(width, width).astype(jnp.bfloat16)
 
-    for group in grouped(half, 4):
+    for group in grouped(half, 4)[:-1] + grouped(half, 2)[-2:]:
         for h in group:
             for copy in loads[h]:
                 copy.wait()
@@ -392,9 +392,10 @@
     got = lax.ppermute(theirs, "core", swap)
     own = block_states(starts, keys, values, False)
     parts = chip_states(own, got, chips)
-    parts = lax.all_to_all(parts, ("outer", "z"), 0, 0, tiled=True)
+    parts = lax.all_to_all(parts.reshape(chips, 1, -1), ("outer", "z"), 0, 0, tiled=True)
+    parts = parts.reshape(-1, width)
     mine, weights, done = inside(starts, lengths, queries, keys, values, scale, False)
-    befores = scan_chips(parts, done)
+    befores = scan_chips(parts, done, chips)
     before = lax.all_to_all(befores, ("outer", "z"), 0, 0, tiled=True)
     rest, _, done = inside(starts, lengths, queries, keys, values, scale, True)
     before = before.reshape(-1, width)

time: 71.8 us -> 70.4 us (0.981)
  waiting for transfers between devices: 8.85 us -> 7.16 us
    all_to_all x1, waiting for transfers between devices: 5.89 us -> 3.57 us  [shards(): lax.all_to_all(parts.reshape(chips, 1, -1), ('outer', 'z'), 0, 0, tiled=T...]
    all_to_all x1, starting transfers between devices: 5.28 us -> 6.22 us  [shards(): before = lax.all_to_all(befores, ('outer', 'z'), 0, 0, tiled=True)]
  transfers between devices with their start and end apart: 4 -> 4, of which waited for: 2 -> 2; matrix products, arithmetic and copies ran while one was open for 0% -> 0% of each run, Pallas kernels for 41% -> 42%
where the time goes in v4:
time: 70.4 us; the launch traced here: 69.8 us
  Pallas kernels  39.5 us (56%)
  starting transfers between devices  21.6 us (31%)
  waiting for transfers between devices  7.16 us (10%)
  between operations  1.54 us (2%)
    pallas_call x2, Pallas kernels, inside(): pl.pallas_call(functools.partial(inside_kernel, heads, scale), out_shape=...  21.6 us
    all_to_all x1, starting transfers between devices, shards(): lax.all_to_all(parts.reshape(chips, 1, -1), ('outer', 'z'), 0, 0, tiled=T...  11.3 us
    pallas_call x2, Pallas kernels, finish(): pl.pallas_call(functools.partial(final_kernel, other), out_shape=pltpu.HB...  9.09 us
    pallas_call x2, Pallas kernels, block_states(): pl.pallas_call(functools.partial(state_kernel, other), out_shape=pltpu.VM...  6.79 us
    all_to_all x1, starting transfers between devices, shards(): before = lax.all_to_all(befores, ('outer', 'z'), 0, 0, tiled=True)  6.22 us
    all_to_all x1, waiting for transfers between devices, shards(): before = lax.all_to_all(befores, ('outer', 'z'), 0, 0, tiled=True)  3.58 us
    all_to_all x1, waiting for transfers between devices, shards(): lax.all_to_all(parts.reshape(chips, 1, -1), ('outer', 'z'), 0, 0, tiled=T...  3.57 us
    ppermute x1, starting transfers between devices, shards(): carried = lax.ppermute(send, 'core', swap)  2.69 us
  transfers between devices with their start and end apart: 4, of which 2 were waited for; matrix products, arithmetic and copies ran while one was open for 0% of the time, Pallas kernels for 42%

profile of v4, /device:TPU:1, one launch (start us, length us, event | category | flops | bytes accessed | tf_op | source)
XLA Modules:
  0.0 69.8 jit_solution(5852415217161746051)
XLA Ops:
  0.7 3.4 %states.3 = f32[1552,128]{1,0:T(8,128)S(1)} custom-call(s32[1]{0:T(128)S(6)} %copy.9.start_ref, bf16[24,1024,128]{2,1,0:T(8,128)(2,1)} %k_hbm.3, bf16[24,1024,128]{2,1,0:T(8,128)(2,1)} %v_hbm.3), custom_call_target="tpu_custom_call" | custom-call | flops 402653184 | bytes 6291456 | tf_op jit(solution)/shard_map/states/pallas_call | solution.py:79
  4.1 1.5 %collective-permute-start = (f32[1552,128]{1,0:T(8,128)S(1)}, f32[1552,128]{1,0:T(8,128)S(1)}, u32[]{:S(2)}, u32[]{:S(2)}) collective-permute-start(f32[1552,128]{1,0:T(8,128)S(1)} %states.3), channel_id=1, source_target_pairs={{0,1},{1,0},{2,3},{3,2},{4,5},{5,4},{6,7},{7,6},{8,9},{9,8},{10,11... | collective-permute-start | bytes 2383880 | tf_op jit(solution)/shard_map/ppermute | solution.py:392
  5.5 3.4 %states.2.own_ref = f32[1552,128]{1,0:T(8,128)S(1)} custom-call(s32[1]{0:T(128)S(6)} %copy.9.start_ref, bf16[24,1024,128]{2,1,0:T(8,128)(2,1)} %k_hbm.3, bf16[24,1024,128]{2,1,0:T(8,128)(2,1)} %v_hbm.3), custom_call_target="tpu_custom_call" | custom-call | flops 402653184 | bytes 6291456 | tf_op jit(solution)/shard_map/states/pallas_call | solution.py:79
  8.9 0.0 collective-permute-done.got_ref.refs_0_
  8.9 1.0 %chip_states.1 = f32[1600,128]{1,0:T(8,128)} custom-call(f32[1552,128]{1,0:T(8,128)S(1)} %states.2.own_ref, f32[1552,128]{1,0:T(8,128)S(1)} %collective-permute-done.got_ref.refs_0_), custom_call_target="tpu_custom_call" | custom-call | tf_op jit(solution)/shard_map/chip_states/pallas_call | solution.py:138
  9.9 11.3 %all-to-all-start = ((f32[64,1,3200]{2,1,0:T(1,128)}), f32[64,1,3200]{2,1,0:T(1,128)S(1)}, u32[]{:S(2)}, u32[]{:S(2)}) async-start(f32[64,1,3200]{2,1,0:T(1,128)} %bitcast.6), calls=%async_computation | async-start | bytes 1638400 | tf_op jit(solution)/shard_map/all_to_all | solution.py:395
  21.8 10.8 %inside.3 = (bf16[12,1024,128]{2,1,0:T(8,128)(2,1)}, f32[1024,128]{1,0:T(8,128)S(1)}, f32[8,128]{1,0:T(8,128)S(1)}) custom-call(s32[1]{0:T(128)S(6)} %copy.9.start_ref, s32[1]{0:T(128)S(6)} %copy.10.length_ref, bf16[24,1024,128]{2,1,0:T(8,128)(2,1)} %q_hbm.3, bf16[24,1024,128]{2,1,0:T(8,128)(2,1)} %k_hbm.3, bf16[24,1024,128]{2,1,0:T(8,128)(2,1)} %v_hbm.3), custom_call_target="tpu_custom_call" | custom-call | flops 2415919104 | bytes 12582912 | tf_op jit(solution)/shard_map/inside/pallas_call | solution.py:275
  32.6 3.6 %all-to-all-done = f32[64,1,3200]{2,1,0:T(1,128)S(1)} async-done(((f32[64,1,3200]{2,1,0:T(1,128)}), f32[64,1,3200]{2,1,0:T(1,128)S(1)}, u32[]{:S(2)}, u32[]{:S(2)}) %all-to-all-start) | async-done | bytes 819232 | tf_op jit(solution)/shard_map/all_to_all | solution.py:395
  36.2 0.9 %scan_chips.1 = f32[64,24,128]{2,1,0:T(8,128)} custom-call(f32[1600,128]{1,0:T(8,128)S(1)} %bitcast.5, f32[8,128]{1,0:T(8,128)S(1)} %get-tuple-element.12.after_ref), custom_call_target="tpu_custom_call" | custom-call | tf_op jit(solution)/shard_map/scan_chips/pallas_call | solution.py:171
  37.1 6.2 %all-to-all-start.1 = ((f32[64,24,128]{2,1,0:T(8,128)}), f32[64,24,128]{2,1,0:T(8,128)S(1)}, u32[]{:S(2)}, u32[]{:S(2)}) async-start(f32[64,24,128]{2,1,0:T(8,128)} %scan_chips.1), calls=%async_computation.1 | async-start | bytes 1572864 | tf_op jit(solution)/shard_map/all_to_all | solution.py:399
  43.4 10.8 %inside.2 = (bf16[12,1024,128]{2,1,0:T(8,128)(2,1)}, f32[1024,128]{1,0:T(8,128)}, f32[8,128]{1,0:T(8,128)S(1)}) custom-call(s32[1]{0:T(128)S(6)} %copy.9.start_ref, s32[1]{0:T(128)S(6)} %copy.10.length_ref, bf16[24,1024,128]{2,1,0:T(8,128)(2,1)} %q_hbm.3, bf16[24,1024,128]{2,1,0:T(8,128)(2,1)} %k_hbm.3, bf16[24,1024,128]{2,1,0:T(8,128)(2,1)} %v_hbm.3), custom_call_target="tpu_custom_call" | custom-call | flops 2415919104 | bytes 12582912 | tf_op jit(solution)/shard_map/inside/pallas_call | solution.py:275
  54.2 3.6 %all-to-all-done.1 = f32[64,24,128]{2,1,0:T(8,128)S(1)} async-done(((f32[64,24,128]{2,1,0:T(8,128)}), f32[64,24,128]{2,1,0:T(8,128)S(1)}, u32[]{:S(2)}, u32[]{:S(2)}) %all-to-all-start.1) | async-done | bytes 786464 | tf_op jit(solution)/shard_map/all_to_all | solution.py:399
  57.8 0.1 carried_to_send.1
  57.9 2.7 %collective-permute-start.1 = (f32[1536,128]{1,0:T(8,128)S(1)}, f32[1536,128]{1,0:T(8,128)S(1)}, u32[]{:S(2)}, u32[]{:S(2)}) collective-permute-start(f32[1536,128]{1,0:T(8,128)S(1)} %carried_to_send.1), channel_id=1, source_target_pairs={{0,1},{1,0},{2,3},{3,2},{4,5},{5,4},{6,7},{7,6},{8,9},{9,8},{10,11... | collective-permute-start | bytes 2359304 | tf_op jit(solution)/shard_map/ppermute | solution.py:403
  60.6 4.5 %finish.2.refs_0_ = bf16[24,1024,128]{2,1,0:T(8,128)(2,1)} custom-call(bf16[24,1024,128]{2,1,0:T(8,128)(2,1)} %q_hbm.3, bf16[12,1024,128]{2,1,0:T(8,128)(2,1)} %get-tuple-element.14.o_hbm, f32[1024,128]{1,0:T(8,128)S(1)} %get-tuple-element.11.w_ref, f32[1536,128]{1,0:T(8,128)S(1)} %bitcast.4, f32[1552,128]{1,0:T(8,128)S(1)} %collective-permute-done.got_ref.refs_0_), custom_call_target="tpu_custom_call" | custom-call | flops 402653184 | bytes 9437184 | tf_op jit(solution)/shard_map/finish/pallas_call | solution.py:361
  65.1 0.0 collective-permute-done.1.carried_ref
  65.1 4.5 %finish.3 = bf16[24,1024,128]{2,1,0:T(8,128)(2,1)} custom-call(bf16[24,1024,128]{2,1,0:T(8,128)(2,1)} %q_hbm.3, bf16[12,1024,128]{2,1,0:T(8,128)(2,1)} %get-tuple-element.10.o_hbm, f32[1024,128]{1,0:T(8,128)S(1)} %get-tuple-element.11.w_ref, f32[1536,128]{1,0:T(8,128)S(1)} %collective-permute-done.1.carried_ref, ...), custom_call_target="tpu_custom_call", output_to_operand_aliasing={{}: (4, {})} | custom-call | flops 402653184 | bytes 9437184 | tf_op jit(solution)/shard_map/finish/pallas_call | solution.py:361
Async XLA Ops:
  4.1 4.9 %collective-permute-start = (f32[1552,128]{1,0:T(8,128)S(1)}, f32[1552,128]{1,0:T(8,128)S(1)}, u32[]{:S(2)}, u32[]{:S(2)}) collective-permute-start(f32[1552,128]{1,0:T(8,128)S(1)} %states.3), channel_id=1, source_target_pairs={{0,1},{1,0},{2,3},{3,2},{4,5},{5,4},{6,7},{7,6},{8,9},{9,8},{10,11... | collective-permute-start | bytes 2383880 | tf_op jit(solution)/shard_map/ppermute | solution.py:392
  9.9 26.3 %all-to-all-start = ((f32[64,1,3200]{2,1,0:T(1,128)}), f32[64,1,3200]{2,1,0:T(1,128)S(1)}, u32[]{:S(2)}, u32[]{:S(2)}) async-start(f32[64,1,3200]{2,1,0:T(1,128)} %bitcast.6), calls=%async_computation | async-start | bytes 1638400 | tf_op jit(solution)/shard_map/all_to_all | solution.py:395
  37.1 20.6 %all-to-all-start.1 = ((f32[64,24,128]{2,1,0:T(8,128)}), f32[64,24,128]{2,1,0:T(8,128)S(1)}, u32[]{:S(2)}, u32[]{:S(2)}) async-start(f32[64,24,128]{2,1,0:T(8,128)} %scan_chips.1), calls=%async_computation.1 | async-start | bytes 1572864 | tf_op jit(solution)/shard_map/all_to_all | solution.py:399
  57.9 7.2 %collective-permute-start.1 = (f32[1536,128]{1,0:T(8,128)S(1)}, f32[1536,128]{1,0:T(8,128)S(1)}, u32[]{:S(2)}, u32[]{:S(2)}) collective-permute-start(f32[1536,128]{1,0:T(8,128)S(1)} %carried_to_send.1), channel_id=1, source_target_pairs={{0,1},{1,0},{2,3},{3,2},{4,5},{5,4},{6,7},{7,6},{8,9},{9,8},{10,11... | collective-permute-start | bytes 2359304 | tf_op jit(solution)/shard_map/ppermute | solution.py:403

commit v5 on v4

--- a/solution.py
+++ b/solution.py
@@ -235,38 +235,39 @@
             pair_ref[i] = jnp.where(allowed, scale, 0.0)
             t = rows_of(low, (CHUNK, width))
             cut = jnp.where(inner, start, low + CHUNK)
-            query_ref[i] = jnp.where(t < cut, 1.0, 0.0)
+            query_ref[i] = jnp.where(t < cut, 1.0, 0.0).astype(query_ref.dtype)
             begin = jnp.where(inner, start, low)
             key_ref[i] = jnp.where(t >= begin, 1.0, 0.0).astype(key_ref.dtype)
 
     start = start_ref[0]
-    for h in range(heads):
-        state = None
-        for i in range(chunks):
-            low = i * CHUNK
-            here = slice(low, low + CHUNK)
+    states = [None] * heads
+    for i in range(chunks):
+        low = i * CHUNK
+        here = slice(low, low + CHUNK)
+        inner = (start >= low) & (start < low + CHUNK)
+        scores = []
+        for h in range(heads):
+            product = lax.dot_general(
+                q_ref[h, here, :],
+                k_ref[h, here, :],
+                (((1,), (1,)), ((), ())),
+                preferred_element_type=jnp.float32,
+            )
+            scores.append((product * pair_ref[i]).astype(jnp.bfloat16))
+        for h in range(heads):
             q, k, v = q_ref[h, here, :], k_ref[h, here, :], v_ref[h, here, :]
-            scores = lax.dot_general(
-                q, k, (((1,), (1,)), ((), ())), preferred_element_type=jnp.float32
-            )
-            scores = (scores * pair_ref[i]).astype(jnp.bfloat16)
-            total = jnp.dot(scores, v, preferred_element_type=jnp.float32)
+            total = jnp.dot(scores[h], v, preferred_element_type=jnp.float32)
             if i > 0:
-                past = (state * scale).astype(jnp.bfloat16)
-                total += jnp.dot(q, past, preferred_element_type=jnp.float32) * query_ref[i]
+                past = (states[h] * scale).astype(jnp.bfloat16)
+                masked = q * query_ref[i]
+                total += jnp.dot(masked, past, preferred_element_type=jnp.float32)
             o_ref[h, here, :] = (total * root_ref[here, :]).astype(o_ref.dtype)
             if i < chunks - 1:
-                new = lax.dot_general(
-                    k * key_ref[i],
-                    v,
-                    (((0,), (0,)), ((), ())),
-                    preferred_element_type=jnp.float32,
-                )
-                inner = (start >= low) & (start < low + CHUNK)
-                state = new if i == 0 else new + state * jnp.where(inner, 0.0, 1.0)
-
-
-def inside(starts, lengths, queries, keys, values, scale, other, heads=2):
+                new = jnp.dot(k.T, v * key_ref[i], preferred_element_type=jnp.float32)
+                states[h] = new if i == 0 else new + states[h] * jnp.where(inner, 0.0, 1.0)
+
+
+def inside(starts, lengths, queries, keys, values, scale, other, heads=4):
     count, rows, width = queries.shape
     chunks = rows // CHUNK
     half = count // 2
@@ -288,11 +289,11 @@
         ),
         scratch_shapes=[
             pltpu.VMEM((chunks, CHUNK, CHUNK), jnp.float32),
-            pltpu.VMEM((chunks, CHUNK, width), jnp.float32),
+            pltpu.VMEM((chunks, CHUNK, width), jnp.bfloat16),
             pltpu.VMEM((chunks, CHUNK, width), jnp.bfloat16),
             pltpu.VMEM((rows, width), jnp.float32),
         ],
-        compiler_params=pltpu.CompilerParams(vmem_limit_bytes=16 * MIB),
+        compiler_params=pltpu.CompilerParams(vmem_limit_bytes=24 * MIB),
         cost_estimate=pl.CostEstimate(
             flops=half * rows * width * (4 * CHUNK + 4 * width),
             bytes_accessed=half * rows * width * 8,

time: 70.4 us -> 69 us (0.980)
  Pallas kernels: 39.5 us -> 36.3 us
  waiting for transfers between devices: 7.16 us -> 9.72 us
    pallas_call x2, Pallas kernels: 21.6 us -> 18.4 us  [inside(): pl.pallas_call(functools.partial(inside_kernel, heads, scale), out_shape=...]
    all_to_all x1, waiting for transfers between devices: 3.57 us -> 5.2 us  [shards(): lax.all_to_all(parts.reshape(chips, 1, -1), ('outer', 'z'), 0, 0, tiled=T...]
    all_to_all x1, starting transfers between devices: 6.22 us -> 5.06 us  [shards(): before = lax.all_to_all(befores, ('outer', 'z'), 0, 0, tiled=True)]
    all_to_all x1, waiting for transfers between devices: 3.58 us -> 4.52 us  [shards(): before = lax.all_to_all(befores, ('outer', 'z'), 0, 0, tiled=True)]
  transfers between devices with their start and end apart: 4 -> 4, of which waited for: 2 -> 2; matrix products, arithmetic and copies ran while one was open for 0% -> 0% of each run, Pallas kernels for 42% -> 38%
where the time goes in v5:
time: 69 us; the launch traced here: 68.7 us
  Pallas kernels  36.3 us (53%)
  starting transfers between devices  21.1 us (31%)
  waiting for transfers between devices  9.72 us (14%)
  between operations  1.54 us (2%)
    pallas_call x2, Pallas kernels, inside(): pl.pallas_call(functools.partial(inside_kernel, heads, scale), out_shape=...  18.4 us
    all_to_all x1, starting transfers between devices, shards(): lax.all_to_all(parts.reshape(chips, 1, -1), ('outer', 'z'), 0, 0, tiled=T...  11.3 us
    pallas_call x2, Pallas kernels, finish(): pl.pallas_call(functools.partial(final_kernel, other), out_shape=pltpu.HB...  9.1 us
    pallas_call x2, Pallas kernels, block_states(): pl.pallas_call(functools.partial(state_kernel, other), out_shape=pltpu.VM...  6.79 us
    all_to_all x1, waiting for transfers between devices, shards(): lax.all_to_all(parts.reshape(chips, 1, -1), ('outer', 'z'), 0, 0, tiled=T...  5.2 us
    all_to_all x1, starting transfers between devices, shards(): before = lax.all_to_all(befores, ('outer', 'z'), 0, 0, tiled=True)  5.06 us
    all_to_all x1, waiting for transfers between devices, shards(): before = lax.all_to_all(befores, ('outer', 'z'), 0, 0, tiled=True)  4.52 us
    ppermute x1, starting transfers between devices, shards(): carried = lax.ppermute(send, 'core', swap)  3.35 us
  transfers between devices with their start and end apart: 4, of which 2 were waited for; matrix products, arithmetic and copies ran while one was open for 0% of the time, Pallas kernels for 38%

profile of v5, /device:TPU:1, one launch (start us, length us, event | category | flops | bytes accessed | tf_op | source)
XLA Modules:
  0.0 68.7 jit_solution(4359314897641389083)
XLA Ops:
  0.7 3.4 %states.3 = f32[1552,128]{1,0:T(8,128)S(1)} custom-call(s32[1]{0:T(128)S(6)} %copy.9.start_ref, bf16[24,1024,128]{2,1,0:T(8,128)(2,1)} %k_hbm.3, bf16[24,1024,128]{2,1,0:T(8,128)(2,1)} %v_hbm.3), custom_call_target="tpu_custom_call" | custom-call | flops 402653184 | bytes 6291456 | tf_op jit(solution)/shard_map/states/pallas_call | solution.py:79
  4.1 1.5 %collective-permute-start = (f32[1552,128]{1,0:T(8,128)S(1)}, f32[1552,128]{1,0:T(8,128)S(1)}, u32[]{:S(2)}, u32[]{:S(2)}) collective-permute-start(f32[1552,128]{1,0:T(8,128)S(1)} %states.3), channel_id=1, source_target_pairs={{0,1},{1,0},{2,3},{3,2},{4,5},{5,4},{6,7},{7,6},{8,9},{9,8},{10,11... | collective-permute-start | bytes 2383880 | tf_op jit(solution)/shard_map/ppermute | solution.py:393
  5.5 3.4 %states.2.own_ref = f32[1552,128]{1,0:T(8,128)S(1)} custom-call(s32[1]{0:T(128)S(6)} %copy.9.start_ref, bf16[24,1024,128]{2,1,0:T(8,128)(2,1)} %k_hbm.3, bf16[24,1024,128]{2,1,0:T(8,128)(2,1)} %v_hbm.3), custom_call_target="tpu_custom_call" | custom-call | flops 402653184 | bytes 6291456 | tf_op jit(solution)/shard_map/states/pallas_call | solution.py:79
  8.9 0.0 collective-permute-done.got_ref.refs_0_
  8.9 1.0 %chip_states.1 = f32[1600,128]{1,0:T(8,128)} custom-call(f32[1552,128]{1,0:T(8,128)S(1)} %states.2.own_ref, f32[1552,128]{1,0:T(8,128)S(1)} %collective-permute-done.got_ref.refs_0_), custom_call_target="tpu_custom_call" | custom-call | tf_op jit(solution)/shard_map/chip_states/pallas_call | solution.py:138
  9.9 11.3 %all-to-all-start = ((f32[64,1,3200]{2,1,0:T(1,128)}), f32[64,1,3200]{2,1,0:T(1,128)S(1)}, u32[]{:S(2)}, u32[]{:S(2)}) async-start(f32[64,1,3200]{2,1,0:T(1,128)} %bitcast.6), calls=%async_computation | async-start | bytes 1638400 | tf_op jit(solution)/shard_map/all_to_all | solution.py:396
  21.8 9.2 %inside.3 = (bf16[12,1024,128]{2,1,0:T(8,128)(2,1)}, f32[1024,128]{1,0:T(8,128)S(1)}, f32[8,128]{1,0:T(8,128)S(1)}) custom-call(s32[1]{0:T(128)S(6)} %copy.9.start_ref, s32[1]{0:T(128)S(6)} %copy.10.length_ref, bf16[24,1024,128]{2,1,0:T(8,128)(2,1)} %q_hbm.3, bf16[24,1024,128]{2,1,0:T(8,128)(2,1)} %k_hbm.3, bf16[24,1024,128]{2,1,0:T(8,128)(2,1)} %v_hbm.3), custom_call_target="tpu_custom_call" | custom-call | flops 2415919104 | bytes 12582912 | tf_op jit(solution)/shard_map/inside/pallas_call | solution.py:276
  31.0 5.2 %all-to-all-done = f32[64,1,3200]{2,1,0:T(1,128)S(1)} async-done(((f32[64,1,3200]{2,1,0:T(1,128)}), f32[64,1,3200]{2,1,0:T(1,128)S(1)}, u32[]{:S(2)}, u32[]{:S(2)}) %all-to-all-start) | async-done | bytes 819232 | tf_op jit(solution)/shard_map/all_to_all | solution.py:396
  36.2 0.9 %scan_chips.1 = f32[64,24,128]{2,1,0:T(8,128)} custom-call(f32[1600,128]{1,0:T(8,128)S(1)} %bitcast.5, f32[8,128]{1,0:T(8,128)S(1)} %get-tuple-element.12.after_ref), custom_call_target="tpu_custom_call" | custom-call | tf_op jit(solution)/shard_map/scan_chips/pallas_call | solution.py:171
  37.1 5.1 %all-to-all-start.1 = ((f32[64,24,128]{2,1,0:T(8,128)}), f32[64,24,128]{2,1,0:T(8,128)S(1)}, u32[]{:S(2)}, u32[]{:S(2)}) async-start(f32[64,24,128]{2,1,0:T(8,128)} %scan_chips.1), calls=%async_computation.1 | async-start | bytes 1572864 | tf_op jit(solution)/shard_map/all_to_all | solution.py:400
  42.2 9.2 %inside.2 = (bf16[12,1024,128]{2,1,0:T(8,128)(2,1)}, f32[1024,128]{1,0:T(8,128)}, f32[8,128]{1,0:T(8,128)S(1)}) custom-call(s32[1]{0:T(128)S(6)} %copy.9.start_ref, s32[1]{0:T(128)S(6)} %copy.10.length_ref, bf16[24,1024,128]{2,1,0:T(8,128)(2,1)} %q_hbm.3, bf16[24,1024,128]{2,1,0:T(8,128)(2,1)} %k_hbm.3, bf16[24,1024,128]{2,1,0:T(8,128)(2,1)} %v_hbm.3), custom_call_target="tpu_custom_call" | custom-call | flops 2415919104 | bytes 12582912 | tf_op jit(solution)/shard_map/inside/pallas_call | solution.py:276
  51.4 4.5 %all-to-all-done.1 = f32[64,24,128]{2,1,0:T(8,128)S(1)} async-done(((f32[64,24,128]{2,1,0:T(8,128)}), f32[64,24,128]{2,1,0:T(8,128)S(1)}, u32[]{:S(2)}, u32[]{:S(2)}) %all-to-all-start.1) | async-done | bytes 786464 | tf_op jit(solution)/shard_map/all_to_all | solution.py:400
  55.9 0.1 carried_to_send.1
  56.1 3.4 %collective-permute-start.1 = (f32[1536,128]{1,0:T(8,128)S(1)}, f32[1536,128]{1,0:T(8,128)S(1)}, u32[]{:S(2)}, u32[]{:S(2)}) collective-permute-start(f32[1536,128]{1,0:T(8,128)S(1)} %carried_to_send.1), channel_id=1, source_target_pairs={{0,1},{1,0},{2,3},{3,2},{4,5},{5,4},{6,7},{7,6},{8,9},{9,8},{10,11... | collective-permute-start | bytes 2359304 | tf_op jit(solution)/shard_map/ppermute | solution.py:404
  59.4 4.5 %finish.2.refs_0_ = bf16[24,1024,128]{2,1,0:T(8,128)(2,1)} custom-call(bf16[24,1024,128]{2,1,0:T(8,128)(2,1)} %q_hbm.3, bf16[12,1024,128]{2,1,0:T(8,128)(2,1)} %get-tuple-element.14.o_hbm, f32[1024,128]{1,0:T(8,128)S(1)} %get-tuple-element.11.w_ref, f32[1536,128]{1,0:T(8,128)S(1)} %bitcast.4, f32[1552,128]{1,0:T(8,128)S(1)} %collective-permute-done.got_ref.refs_0_), custom_call_target="tpu_custom_call" | custom-call | flops 402653184 | bytes 9437184 | tf_op jit(solution)/shard_map/finish/pallas_call | solution.py:362
  64.0 0.0 collective-permute-done.1.carried_ref
  64.0 4.5 %finish.3 = bf16[24,1024,128]{2,1,0:T(8,128)(2,1)} custom-call(bf16[24,1024,128]{2,1,0:T(8,128)(2,1)} %q_hbm.3, bf16[12,1024,128]{2,1,0:T(8,128)(2,1)} %get-tuple-element.10.o_hbm, f32[1024,128]{1,0:T(8,128)S(1)} %get-tuple-element.11.w_ref, f32[1536,128]{1,0:T(8,128)S(1)} %collective-permute-done.1.carried_ref, ...), custom_call_target="tpu_custom_call", output_to_operand_aliasing={{}: (4, {})} | custom-call | flops 402653184 | bytes 9437184 | tf_op jit(solution)/shard_map/finish/pallas_call | solution.py:362
Async XLA Ops:
  4.1 4.9 %collective-permute-start = (f32[1552,128]{1,0:T(8,128)S(1)}, f32[1552,128]{1,0:T(8,128)S(1)}, u32[]{:S(2)}, u32[]{:S(2)}) collective-permute-start(f32[1552,128]{1,0:T(8,128)S(1)} %states.3), channel_id=1, source_target_pairs={{0,1},{1,0},{2,3},{3,2},{4,5},{5,4},{6,7},{7,6},{8,9},{9,8},{10,11... | collective-permute-start | bytes 2383880 | tf_op jit(solution)/shard_map/ppermute | solution.py:393
  9.9 26.3 %all-to-all-start = ((f32[64,1,3200]{2,1,0:T(1,128)}), f32[64,1,3200]{2,1,0:T(1,128)S(1)}, u32[]{:S(2)}, u32[]{:S(2)}) async-start(f32[64,1,3200]{2,1,0:T(1,128)} %bitcast.6), calls=%async_computation | async-start | bytes 1638400 | tf_op jit(solution)/shard_map/all_to_all | solution.py:396
  37.1 18.8 %all-to-all-start.1 = ((f32[64,24,128]{2,1,0:T(8,128)}), f32[64,24,128]{2,1,0:T(8,128)S(1)}, u32[]{:S(2)}, u32[]{:S(2)}) async-start(f32[64,24,128]{2,1,0:T(8,128)} %scan_chips.1), calls=%async_computation.1 | async-start | bytes 1572864 | tf_op jit(solution)/shard_map/all_to_all | solution.py:400
  56.1 7.9 %collective-permute-start.1 = (f32[1536,128]{1,0:T(8,128)S(1)}, f32[1536,128]{1,0:T(8,128)S(1)}, u32[]{:S(2)}, u32[]{:S(2)}) collective-permute-start(f32[1536,128]{1,0:T(8,128)S(1)} %carried_to_send.1), channel_id=1, source_target_pairs={{0,1},{1,0},{2,3},{3,2},{4,5},{5,4},{6,7},{7,6},{8,9},{9,8},{10,11... | collective-permute-start | bytes 2359304 | tf_op jit(solution)/shard_map/ppermute | solution.py:404

commit v6 on v5

--- a/solution.py
+++ b/solution.py
@@ -303,24 +303,27 @@
     )(starts, lengths, in_hbm(queries), in_hbm(keys), in_hbm(values))
 
 
-def final_kernel(other, q_hbm, o_hbm, w_ref, carried_ref, *refs):
+def final_kernel(other, *refs):
     if other:
-        _, out_hbm, q_ref, o_ref, made_ref, q_sems, o_sems, out_sems = refs
+        q_ref, o_ref, w_ref, carried_ref, _, out_hbm, made_ref, out_sems = refs
     else:
-        got_ref, out_hbm, q_ref, o_ref, made_ref, q_sems, o_sems, out_sems = refs
+        q_hbm, o_hbm, rest_hbm, w_ref, carried_ref, got_ref, out_hbm, next_q_ref, next_o_ref = refs[:9]
+        q_ref, o_ref, made_ref, out_sems, q_sems, o_sems, next_q_sems, next_o_sems = refs[9:]
         reset, mate = marks(got_ref)
         kept, added = 1.0 - mate * reset, mate
-    half, rows, width = q_ref.shape
+    half, rows, width = made_ref.shape
     base = half_of(other) * half
-    loads, stores = [], []
-    for h in range(half):
-        pair = (
-            pltpu.make_async_copy(q_hbm.at[base + h], q_ref.at[h], q_sems.at[h]),
-            pltpu.make_async_copy(o_hbm.at[h], o_ref.at[h], o_sems.at[h]),
-        )
-        for copy in pair:
-            copy.start()
-        loads.append(pair)
+    loads, pending = [], []
+    if not other:
+        next_base = half_of(True) * half
+        for h in range(half):
+            pair = (
+                pltpu.make_async_copy(q_hbm.at[base + h], q_ref.at[h], q_sems.at[h]),
+                pltpu.make_async_copy(o_hbm.at[h], o_ref.at[h], o_sems.at[h]),
+            )
+            for copy in pair:
+                copy.start()
+            loads.append(pair)
     nothing = jnp.zeros((width, width), jnp.bfloat16)
 
     def carried(h):
@@ -330,10 +333,21 @@
             total = tiles(total) * kept[None] + tiles(got_ref[here, :]) * added[None]
         return total.reshape(width, width).astype(jnp.bfloat16)
 
-    for group in grouped(half, 4)[:-1] + grouped(half, 2)[-2:]:
-        for h in group:
-            for copy in loads[h]:
-                copy.wait()
+    fours = [range(h, h + 4) for h in range(2, half - 2, 4)]
+    for group in [range(2), *fours, range(half - 2, half)]:
+        if not other:
+            for h in group:
+                for copy in loads[h]:
+                    copy.wait()
+            for h in group:
+                for copy in (
+                    pltpu.make_async_copy(
+                        q_hbm.at[next_base + h], next_q_ref.at[h], next_q_sems.at[h]
+                    ),
+                    pltpu.make_async_copy(rest_hbm.at[h], next_o_ref.at[h], next_o_sems.at[h]),
+                ):
+                    copy.start()
+                    pending.append(copy)
         for h in group[::2]:
             both = jnp.concatenate(
                 [
@@ -351,36 +365,59 @@
         for h in group:
             store = pltpu.make_async_copy(made_ref.at[h], out_hbm.at[base + h], out_sems.at[h])
             store.start()
-            stores.append(store)
-    for store in stores:
-        store.wait()
-
-
-def finish(queries, partial, weights, carried, other, extra):
+            pending.append(store)
+    for copy in pending:
+        copy.wait()
+
+
+def finish_own(queries, partial, rest, weights, before, got):
     count, rows, width = queries.shape
     half = count // 2
-    return pl.pallas_call(
-        functools.partial(final_kernel, other),
-        out_shape=pltpu.HBM(queries.shape, jnp.bfloat16),
-        in_specs=[ANYWHERE, ANYWHERE, WHOLE, WHOLE, ANYWHERE if other else WHOLE],
-        out_specs=ANYWHERE,
+    fetched = pltpu.VMEM((half, rows, width), jnp.bfloat16)
+    return pl.pallas_call(
+        functools.partial(final_kernel, False),
+        out_shape=(pltpu.HBM(queries.shape, jnp.bfloat16), fetched, fetched),
+        in_specs=[ANYWHERE] * 3 + [WHOLE] * 3,
+        out_specs=(ANYWHERE, WHOLE, WHOLE),
         scratch_shapes=[pltpu.VMEM((half, rows, width), jnp.bfloat16)] * 3
-        + [pltpu.SemaphoreType.DMA((half,))] * 3,
-        input_output_aliases={4: 0} if other else {},
+        + [pltpu.SemaphoreType.DMA((half,))] * 5,
         compiler_params=pltpu.CompilerParams(vmem_limit_bytes=16 * MIB),
         cost_estimate=pl.CostEstimate(
             flops=2 * half * rows * width * width,
-            bytes_accessed=half * rows * width * 6,
+            bytes_accessed=half * rows * width * 10,
             transcendentals=0,
         ),
-        name="finish",
+        name="finish_own",
     )(
         in_hbm(queries),
         in_hbm(partial),
+        in_hbm(rest),
         in_vmem(weights),
-        in_vmem(carried),
-        in_hbm(extra) if other else in_vmem(extra),
+        in_vmem(before),
+        in_vmem(got),
     )
+
+
+def finish_rest(queries, partial, weights, carried, out):
+    half, rows, width = queries.shape
+    return pl.pallas_call(
+        functools.partial(final_kernel, True),
+        out_shape=pltpu.HBM(out.shape, jnp.bfloat16),
+        in_specs=[WHOLE] * 4 + [ANYWHERE],
+        out_specs=ANYWHERE,
+        scratch_shapes=[
+            pltpu.VMEM((half, rows, width), jnp.bfloat16),
+            pltpu.SemaphoreType.DMA((half,)),
+        ],
+        input_output_aliases={4: 0},
+        compiler_params=pltpu.CompilerParams(vmem_limit_bytes=16 * MIB),
+        cost_estimate=pl.CostEstimate(
+            flops=2 * half * rows * width * width,
+            bytes_accessed=half * rows * width * 2,
+            transcendentals=0,
+        ),
+        name="finish_rest",
+    )(in_vmem(queries), in_vmem(partial), in_vmem(weights), in_vmem(carried), in_hbm(out))
 
 
 def shards(queries, keys, values, starts, lengths):
@@ -402,8 +439,8 @@
     before = before.reshape(-1, width)
     send = carried_to_send(before, own, done)
     carried = lax.ppermute(send, "core", swap)
-    out = finish(queries, mine, weights, before, False, got)
-    return finish(queries, rest, weights, carried, True, out)
+    out, rest_q, rest_o = finish_own(queries, mine, rest, weights, before, got)
+    return finish_rest(rest_q, rest_o, weights, carried, out)
 
 
 def solution(mesh):

time: 69 us -> 68.7 us (level)
  transfers between devices with their start and end apart: 4 -> 4, of which waited for: 2 -> 2; matrix products, arithmetic and copies ran while one was open for 0% -> 0% of each run, Pallas kernels for 38% -> 41%
where the time goes in v6:
time: 68.7 us; the launch traced here: 68.3 us
  Pallas kernels  35.9 us (52%)
  starting transfers between devices  21.1 us (31%)
  waiting for transfers between devices  9.73 us (14%)
  between operations  1.54 us (2%)
    pallas_call x2, Pallas kernels, inside(): pl.pallas_call(functools.partial(inside_kernel, heads, scale), out_shape=...  18.4 us
    all_to_all x1, starting transfers between devices, shards(): lax.all_to_all(parts.reshape(chips, 1, -1), ('outer', 'z'), 0, 0, tiled=T...  11.3 us
    pallas_call x2, Pallas kernels, block_states(): pl.pallas_call(functools.partial(state_kernel, other), out_shape=pltpu.VM...  6.79 us
    pallas_call x1, Pallas kernels, finish_own(): pl.pallas_call(functools.partial(final_kernel, False), out_shape=(pltpu.H...  6.34 us
    all_to_all x1, waiting for transfers between devices, shards(): lax.all_to_all(parts.reshape(chips, 1, -1), ('outer', 'z'), 0, 0, tiled=T...  5.2 us
    all_to_all x1, starting transfers between devices, shards(): before = lax.all_to_all(befores, ('outer', 'z'), 0, 0, tiled=True)  5.06 us
    all_to_all x1, waiting for transfers between devices, shards(): before = lax.all_to_all(befores, ('outer', 'z'), 0, 0, tiled=True)  4.52 us
    ppermute x1, starting transfers between devices, shards(): carried = lax.ppermute(send, 'core', swap)  3.35 us
  transfers between devices with their start and end apart: 4, of which 2 were waited for; matrix products, arithmetic and copies ran while one was open for 0% of the time, Pallas kernels for 41%

profile of v6, /device:TPU:1, one launch (start us, length us, event | category | flops | bytes accessed | tf_op | source)
XLA Modules:
  0.0 68.3 jit_solution(13024093291916711497)
XLA Ops:
  0.7 3.4 %states.3 = f32[1552,128]{1,0:T(8,128)S(1)} custom-call(s32[1]{0:T(128)S(6)} %copy.9.start_ref, bf16[24,1024,128]{2,1,0:T(8,128)(2,1)} %k_hbm.3, bf16[24,1024,128]{2,1,0:T(8,128)(2,1)} %v_hbm.3), custom_call_target="tpu_custom_call" | custom-call | flops 402653184 | bytes 6291456 | tf_op jit(solution)/shard_map/states/pallas_call | solution.py:79
  4.1 1.5 %collective-permute-start = (f32[1552,128]{1,0:T(8,128)S(1)}, f32[1552,128]{1,0:T(8,128)S(1)}, u32[]{:S(2)}, u32[]{:S(2)}) collective-permute-start(f32[1552,128]{1,0:T(8,128)S(1)} %states.3), channel_id=1, source_target_pairs={{0,1},{1,0},{2,3},{3,2},{4,5},{5,4},{6,7},{7,6},{8,9},{9,8},{10,11... | collective-permute-start | bytes 2383880 | tf_op jit(solution)/shard_map/ppermute | solution.py:430
  5.5 3.4 %states.2.own_ref = f32[1552,128]{1,0:T(8,128)S(1)} custom-call(s32[1]{0:T(128)S(6)} %copy.9.start_ref, bf16[24,1024,128]{2,1,0:T(8,128)(2,1)} %k_hbm.3, bf16[24,1024,128]{2,1,0:T(8,128)(2,1)} %v_hbm.3), custom_call_target="tpu_custom_call" | custom-call | flops 402653184 | bytes 6291456 | tf_op jit(solution)/shard_map/states/pallas_call | solution.py:79
  8.9 0.0 collective-permute-done.got_ref.refs_5_
  8.9 1.0 %chip_states.1 = f32[1600,128]{1,0:T(8,128)} custom-call(f32[1552,128]{1,0:T(8,128)S(1)} %states.2.own_ref, f32[1552,128]{1,0:T(8,128)S(1)} %collective-permute-done.got_ref.refs_5_), custom_call_target="tpu_custom_call" | custom-call | tf_op jit(solution)/shard_map/chip_states/pallas_call | solution.py:138
  9.9 11.3 %all-to-all-start = ((f32[64,1,3200]{2,1,0:T(1,128)}), f32[64,1,3200]{2,1,0:T(1,128)S(1)}, u32[]{:S(2)}, u32[]{:S(2)}) async-start(f32[64,1,3200]{2,1,0:T(1,128)} %bitcast.6), calls=%async_computation | async-start | bytes 1638400 | tf_op jit(solution)/shard_map/all_to_all | solution.py:433
  21.8 9.2 %inside.2 = (bf16[12,1024,128]{2,1,0:T(8,128)(2,1)}, f32[1024,128]{1,0:T(8,128)S(1)}, f32[8,128]{1,0:T(8,128)S(1)}) custom-call(s32[1]{0:T(128)S(6)} %copy.9.start_ref, s32[1]{0:T(128)S(6)} %copy.10.length_ref, bf16[24,1024,128]{2,1,0:T(8,128)(2,1)} %refs_0_.1, bf16[24,1024,128]{2,1,0:T(8,128)(2,1)} %k_hbm.3, bf16[24,1024,128]{2,1,0:T(8,128)(2,1)} %v_hbm.3), custom_call_target="tpu_custom_call" | custom-call | flops 2415919104 | bytes 12582912 | tf_op jit(solution)/shard_map/inside/pallas_call | solution.py:276
  31.0 5.2 %all-to-all-done = f32[64,1,3200]{2,1,0:T(1,128)S(1)} async-done(((f32[64,1,3200]{2,1,0:T(1,128)}), f32[64,1,3200]{2,1,0:T(1,128)S(1)}, u32[]{:S(2)}, u32[]{:S(2)}) %all-to-all-start) | async-done | bytes 819232 | tf_op jit(solution)/shard_map/all_to_all | solution.py:433
  36.2 0.9 %scan_chips.1 = f32[64,24,128]{2,1,0:T(8,128)} custom-call(f32[1600,128]{1,0:T(8,128)S(1)} %bitcast.5, f32[8,128]{1,0:T(8,128)S(1)} %get-tuple-element.16.after_ref), custom_call_target="tpu_custom_call" | custom-call | tf_op jit(solution)/shard_map/scan_chips/pallas_call | solution.py:171
  37.1 5.1 %all-to-all-start.1 = ((f32[64,24,128]{2,1,0:T(8,128)}), f32[64,24,128]{2,1,0:T(8,128)S(1)}, u32[]{:S(2)}, u32[]{:S(2)}) async-start(f32[64,24,128]{2,1,0:T(8,128)} %scan_chips.1), calls=%async_computation.1 | async-start | bytes 1572864 | tf_op jit(solution)/shard_map/all_to_all | solution.py:437
  42.2 9.2 %inside.3 = (bf16[12,1024,128]{2,1,0:T(8,128)(2,1)}, f32[1024,128]{1,0:T(8,128)}, f32[8,128]{1,0:T(8,128)S(1)}) custom-call(s32[1]{0:T(128)S(6)} %copy.9.start_ref, s32[1]{0:T(128)S(6)} %copy.10.length_ref, bf16[24,1024,128]{2,1,0:T(8,128)(2,1)} %refs_0_.1, bf16[24,1024,128]{2,1,0:T(8,128)(2,1)} %k_hbm.3, bf16[24,1024,128]{2,1,0:T(8,128)(2,1)} %v_hbm.3), custom_call_target="tpu_custom_call" | custom-call | flops 2415919104 | bytes 12582912 | tf_op jit(solution)/shard_map/inside/pallas_call | solution.py:276
  51.4 4.5 %all-to-all-done.1 = f32[64,24,128]{2,1,0:T(8,128)S(1)} async-done(((f32[64,24,128]{2,1,0:T(8,128)}), f32[64,24,128]{2,1,0:T(8,128)S(1)}, u32[]{:S(2)}, u32[]{:S(2)}) %all-to-all-start.1) | async-done | bytes 786464 | tf_op jit(solution)/shard_map/all_to_all | solution.py:437
  55.9 0.1 carried_to_send.1
  56.1 3.4 %collective-permute-start.1 = (f32[1536,128]{1,0:T(8,128)S(1)}, f32[1536,128]{1,0:T(8,128)S(1)}, u32[]{:S(2)}, u32[]{:S(2)}) collective-permute-start(f32[1536,128]{1,0:T(8,128)S(1)} %carried_to_send.1), channel_id=1, source_target_pairs={{0,1},{1,0},{2,3},{3,2},{4,5},{5,4},{6,7},{7,6},{8,9},{9,8},{10,11... | collective-permute-start | bytes 2359304 | tf_op jit(solution)/shard_map/ppermute | solution.py:441
  59.4 6.3 %finish_own.1 = (bf16[24,1024,128]{2,1,0:T(8,128)(2,1)}, bf16[12,1024,128]{2,1,0:T(8,128)(2,1)S(1)}, bf16[12,1024,128]{2,1,0:T(8,128)(2,1)S(1)}) custom-call(bf16[24,1024,128]{2,1,0:T(8,128)(2,1)} %refs_0_.1, bf16[12,1024,128]{2,1,0:T(8,128)(2,1)} %get-tuple-element.13.refs_1_, bf16[12,1024,128]{2,1,0:T(8,128)(2,1)} %get-tuple-element.14.refs_2_, ...), custom_call_target="tpu_custom_call" | custom-call | flops 402653184 | bytes 15728640 | tf_op jit(solution)/shard_map/finish_own/pallas_call | solution.py:377
  65.8 0.0 collective-permute-done.1.refs_3_
  65.8 2.4 %finish_rest.1 = bf16[24,1024,128]{2,1,0:T(8,128)(2,1)} custom-call(bf16[12,1024,128]{2,1,0:T(8,128)(2,1)S(1)} %get-tuple-element.17.refs_0_, bf16[12,1024,128]{2,1,0:T(8,128)(2,1)S(1)} %get-tuple-element.18.refs_1_, f32[1024,128]{1,0:T(8,128)S(1)} %get-tuple-element.15.refs_3_.refs_2_, ...), custom_call_target="tpu_custom_call", output_to_operand_aliasing={{}: (4, {})} | custom-call | flops 402653184 | bytes 3145728 | tf_op jit(solution)/shard_map/finish_rest/pallas_call | solution.py:403
Async XLA Ops:
  4.1 4.9 %collective-permute-start = (f32[1552,128]{1,0:T(8,128)S(1)}, f32[1552,128]{1,0:T(8,128)S(1)}, u32[]{:S(2)}, u32[]{:S(2)}) collective-permute-start(f32[1552,128]{1,0:T(8,128)S(1)} %states.3), channel_id=1, source_target_pairs={{0,1},{1,0},{2,3},{3,2},{4,5},{5,4},{6,7},{7,6},{8,9},{9,8},{10,11... | collective-permute-start | bytes 2383880 | tf_op jit(solution)/shard_map/ppermute | solution.py:430
  9.9 26.3 %all-to-all-start = ((f32[64,1,3200]{2,1,0:T(1,128)}), f32[64,1,3200]{2,1,0:T(1,128)S(1)}, u32[]{:S(2)}, u32[]{:S(2)}) async-start(f32[64,1,3200]{2,1,0:T(1,128)} %bitcast.6), calls=%async_computation | async-start | bytes 1638400 | tf_op jit(solution)/shard_map/all_to_all | solution.py:433
  37.1 18.8 %all-to-all-start.1 = ((f32[64,24,128]{2,1,0:T(8,128)}), f32[64,24,128]{2,1,0:T(8,128)S(1)}, u32[]{:S(2)}, u32[]{:S(2)}) async-start(f32[64,24,128]{2,1,0:T(8,128)} %scan_chips.1), calls=%async_computation.1 | async-start | bytes 1572864 | tf_op jit(solution)/shard_map/all_to_all | solution.py:437
  56.1 9.7 %collective-permute-start.1 = (f32[1536,128]{1,0:T(8,128)S(1)}, f32[1536,128]{1,0:T(8,128)S(1)}, u32[]{:S(2)}, u32[]{:S(2)}) collective-permute-start(f32[1536,128]{1,0:T(8,128)S(1)} %carried_to_send.1), channel_id=1, source_target_pairs={{0,1},{1,0},{2,3},{3,2},{4,5},{5,4},{6,7},{7,6},{8,9},{9,8},{10,11... | collective-permute-start | bytes 2359304 | tf_op jit(solution)/shard_map/ppermute | solution.py:441
